TPU v7x, 32 devices: a whole 2x2x4 slice. The times are simulated.
32 devices in a mesh: dp: 2 (over x), ind: 4 (over z), probe: 4 (over y, core).
Axes of the slice: x: 2, y: 2, z: 4, core: 2. Of those that a mesh axis runs over, the one named last changes fastest.
Arguments:
- data_x: bfloat16 [16, 1024], P(None, 'dp'), may hold values from -6 to 6
- inducing_z: bfloat16 [16, 65536], P(None, 'ind'), may hold values from -6 to 6
- lengthscale: float32 [16], replicated, may hold values from 1.5 to 3
- noise_var: float32 [1], replicated, may hold values from 0.5 to 2
- solves: bfloat16 [32, 65536], P('probe', 'ind'), may hold values from -0.09375 to 0.09375
- probe_signs: int32 [32, 65536], P('probe', 'ind'), may hold values 0 or 1
Outputs:
- grad_z: float32 [16, 65536], P(None, 'ind')
All inputs are finite; a program needn't handle non-finite values. No bound on the sum of `probe_signs` on one device may be relied on, other than what follows from the above.
Results may differ from a plain program's by a relative error of at most 0.0095.
Values may be sent and summed in bfloat16 or wider, within the bound.
No kernel may reach another device: no remote copies, remote signals or barrier semaphores. Data moves between devices by JAX's collectives and lax.ppermute only.
A program may use at most 64 MiB of HBM per device.

v0:
```python
import jax
import jax.numpy as jnp
from jax import lax
from jax.sharding import PartitionSpec as P

P_SIZE = 32


def kernel_block(x_scaled, x_square, z_scaled, z_square):
    cross = lax.dot_general(
        x_scaled, z_scaled, (((0,), (0,)), ((), ())), preferred_element_type=jnp.float32
    )
    dist = x_square[:, None] + z_square[None, :] - 2.0 * cross
    return jnp.exp(-0.5 * dist).astype(jnp.bfloat16)


def on_device(data_x, inducing_z, lengthscale, noise_var, solves, probe_signs):
    probe_vals = (2 * probe_signs - 1).astype(jnp.bfloat16)
    stacked = jnp.concatenate([solves, probe_vals], axis=0)
    half_rows = stacked.shape[0] // 2
    inverse = 1.0 / lengthscale
    x_scaled = (data_x.astype(jnp.float32) * inverse[:, None]).astype(jnp.bfloat16)
    z_scaled = (inducing_z.astype(jnp.float32) * inverse[:, None]).astype(jnp.bfloat16)
    x_wide = x_scaled.astype(jnp.float32)
    z_wide = z_scaled.astype(jnp.float32)
    x_square = jnp.sum(x_wide * x_wide, axis=0)
    z_square = jnp.sum(z_wide * z_wide, axis=0)
    total_cols = z_scaled.shape[1]
    block_cols = min(2048, total_cols)
    blocks_count = total_cols // block_cols
    rows_count = x_scaled.shape[1]

    def first_pass(col_index, totals):
        start = col_index * block_cols
        z_part = lax.dynamic_slice_in_dim(z_scaled, start, block_cols, 1)
        zsq_part = lax.dynamic_slice_in_dim(z_square, start, block_cols, 0)
        kern = kernel_block(x_scaled, x_square, z_part, zsq_part)
        stack_part = lax.dynamic_slice_in_dim(stacked, start, block_cols, 1)
        return totals + lax.dot_general(
            stack_part, kern, (((1,), (1,)), ((), ())), preferred_element_type=jnp.float32
        )

    partial_proj = lax.fori_loop(
        0, blocks_count, first_pass, jnp.zeros((2 * half_rows, rows_count), jnp.float32)
    )
    projections = lax.psum(partial_proj.astype(jnp.bfloat16), "ind")
    swapped = jnp.concatenate([projections[half_rows:], projections[:half_rows]], axis=0)

    def second_pass(col_index, result):
        start = col_index * block_cols
        z_part = lax.dynamic_slice_in_dim(z_scaled, start, block_cols, 1)
        zsq_part = lax.dynamic_slice_in_dim(z_square, start, block_cols, 0)
        kern = kernel_block(x_scaled, x_square, z_part, zsq_part)
        stack_part = lax.dynamic_slice_in_dim(stacked, start, block_cols, 1)
        coef = lax.dot_general(
            swapped, stack_part, (((0,), (0,)), ((), ())), preferred_element_type=jnp.float32
        )
        weighted = (kern.astype(jnp.float32) * coef).astype(jnp.bfloat16)
        moment = jnp.dot(data_x, weighted, preferred_element_type=jnp.float32)
        row_total = jnp.sum(weighted, axis=0, dtype=jnp.float32)
        z_raw = lax.dynamic_slice_in_dim(inducing_z, start, block_cols, 1).astype(jnp.float32)
        return lax.dynamic_update_slice_in_dim(
            result, moment - z_raw * row_total[None, :], start, 1
        )

    partial_grad = lax.fori_loop(
        0, blocks_count, second_pass, jnp.zeros((x_scaled.shape[0], total_cols), jnp.float32)
    )
    summed = lax.psum(partial_grad, ("dp", "probe"))
    factor = inverse * inverse / (noise_var[0] * P_SIZE)
    return summed * factor[:, None]


def solution(mesh):
    return jax.shard_map(
        on_device,
        mesh=mesh,
        in_specs=(P(None, "dp"), P(None, "ind"), P(), P(), P("probe", "ind"), P("probe", "ind")),
        out_specs=P(None, "ind"),
        check_vma=False,
    )
```

profile of v0, /device:TPU:0, one launch (start us, length us, event | category | flops | bytes accessed | tf_op | source)
XLA Modules:
  0.0 134.0 jit_solution(3839862775014209474)
XLA Ops:
  6.5 0.0 copy-start.2
  6.5 0.0 all-reduce.2.cloned.1.call-start
  7.2 1.1 add_convert_fusion
  8.3 0.7 multiply_divide_fusion
  9.0 0.8 multiply_reduce_fusion.1
  9.8 1.4 %multiply_reduce_fusion = (f32[16384]{0:T(1024)S(1)}, bf16[16,16384]{1,0:T(8,128)(2,1)S(1)}) fusion(f32[16]{0:T(128)S(1)} %get-tuple-element.359, bf16[16,16384]{1,0:T(8,128)(2,1)} %param.11), kind=kLoop, calls=%fused_computation.25 | loop fusion | flops 1556480 | bytes 1114176 | tf_op jit(solution)/shard_map/reduce_sum | solution.py:27
  11.2 0.0 copy-done.2
  11.3 0.0 copy-start.1
  11.3 11.8 %while.28 = (s32[]{:T(128)}, f32[16,512]{1,0:T(8,128)S(1)}, bf16[16,16384]{1,0:T(8,128)(2,1)S(1)}, f32[512]{0:T(512)S(1)}, f32[16384]{0:T(1024)S(1)}, /*index=5*...) while((s32[]{:T(128)}, f32[16,512]{1,0:T(8,128)S(1)}, ...), condition=%wide.region_3.0_spmd.clone, body=%wide.region_2.0_spmd.clone.sunk | while | flops 72368136 | bytes 241328 | solution.py:43
  11.3 1.5 %fusion.49 = f32[16,512]{1,0:T(8,128)S(1)} fusion(bf16[16,512]{1,0:T(8,128)(2,1)S(1)} %get-tuple-element.504, f32[2048]{0:T(1024)S(1)} %dynamic_slice.77, f32[512]{0:T(512)S(1)} %get-tuple-element.501, bf16[16,16384]{1,0:T(8,128)(2,1)S(1)} %get-tuple-element.503, s32[]{:T(128)S(6)} %select_n.24, bf16[16,16384]{1,0:T(8,128)(2,1)S(1)} %get-tuple-element.500, ...), kind=kOutput, calls=%fused_computation.19.clone.1 | convolution fusion | flops 72368128 | bytes 224768 | tf_op jit(solution)/shard_map/while/body/eval_jaxpr/dot_general | solution.py:39
  12.8 1.5 %fusion.49 = f32[16,512]{1,0:T(8,128)S(1)} fusion(bf16[16,512]{1,0:T(8,128)(2,1)S(1)} %get-tuple-element.504, f32[2048]{0:T(1024)S(1)} %dynamic_slice.77, f32[512]{0:T(512)S(1)} %get-tuple-element.501, bf16[16,16384]{1,0:T(8,128)(2,1)S(1)} %get-tuple-element.503, s32[]{:T(128)S(6)} %select_n.24, bf16[16,16384]{1,0:T(8,128)(2,1)S(1)} %get-tuple-element.500, ...), kind=kOutput, calls=%fused_computation.19.clone.1 | convolution fusion | flops 72368128 | bytes 224768 | tf_op jit(solution)/shard_map/while/body/eval_jaxpr/dot_general | solution.py:39
  14.2 1.5 %fusion.49 = f32[16,512]{1,0:T(8,128)S(1)} fusion(bf16[16,512]{1,0:T(8,128)(2,1)S(1)} %get-tuple-element.504, f32[2048]{0:T(1024)S(1)} %dynamic_slice.77, f32[512]{0:T(512)S(1)} %get-tuple-element.501, bf16[16,16384]{1,0:T(8,128)(2,1)S(1)} %get-tuple-element.503, s32[]{:T(128)S(6)} %select_n.24, bf16[16,16384]{1,0:T(8,128)(2,1)S(1)} %get-tuple-element.500, ...), kind=kOutput, calls=%fused_computation.19.clone.1 | convolution fusion | flops 72368128 | bytes 224768 | tf_op jit(solution)/shard_map/while/body/eval_jaxpr/dot_general | solution.py:39
  15.7 1.5 %fusion.49 = f32[16,512]{1,0:T(8,128)S(1)} fusion(bf16[16,512]{1,0:T(8,128)(2,1)S(1)} %get-tuple-element.504, f32[2048]{0:T(1024)S(1)} %dynamic_slice.77, f32[512]{0:T(512)S(1)} %get-tuple-element.501, bf16[16,16384]{1,0:T(8,128)(2,1)S(1)} %get-tuple-element.503, s32[]{:T(128)S(6)} %select_n.24, bf16[16,16384]{1,0:T(8,128)(2,1)S(1)} %get-tuple-element.500, ...), kind=kOutput, calls=%fused_computation.19.clone.1 | convolution fusion | flops 72368128 | bytes 224768 | tf_op jit(solution)/shard_map/while/body/eval_jaxpr/dot_general | solution.py:39
  17.2 1.5 %fusion.49 = f32[16,512]{1,0:T(8,128)S(1)} fusion(bf16[16,512]{1,0:T(8,128)(2,1)S(1)} %get-tuple-element.504, f32[2048]{0:T(1024)S(1)} %dynamic_slice.77, f32[512]{0:T(512)S(1)} %get-tuple-element.501, bf16[16,16384]{1,0:T(8,128)(2,1)S(1)} %get-tuple-element.503, s32[]{:T(128)S(6)} %select_n.24, bf16[16,16384]{1,0:T(8,128)(2,1)S(1)} %get-tuple-element.500, ...), kind=kOutput, calls=%fused_computation.19.clone.1 | convolution fusion | flops 72368128 | bytes 224768 | tf_op jit(solution)/shard_map/while/body/eval_jaxpr/dot_general | solution.py:39
  18.7 1.5 %fusion.49 = f32[16,512]{1,0:T(8,128)S(1)} fusion(bf16[16,512]{1,0:T(8,128)(2,1)S(1)} %get-tuple-element.504, f32[2048]{0:T(1024)S(1)} %dynamic_slice.77, f32[512]{0:T(512)S(1)} %get-tuple-element.501, bf16[16,16384]{1,0:T(8,128)(2,1)S(1)} %get-tuple-element.503, s32[]{:T(128)S(6)} %select_n.24, bf16[16,16384]{1,0:T(8,128)(2,1)S(1)} %get-tuple-element.500, ...), kind=kOutput, calls=%fused_computation.19.clone.1 | convolution fusion | flops 72368128 | bytes 224768 | tf_op jit(solution)/shard_map/while/body/eval_jaxpr/dot_general | solution.py:39
  20.1 1.5 %fusion.49 = f32[16,512]{1,0:T(8,128)S(1)} fusion(bf16[16,512]{1,0:T(8,128)(2,1)S(1)} %get-tuple-element.504, f32[2048]{0:T(1024)S(1)} %dynamic_slice.77, f32[512]{0:T(512)S(1)} %get-tuple-element.501, bf16[16,16384]{1,0:T(8,128)(2,1)S(1)} %get-tuple-element.503, s32[]{:T(128)S(6)} %select_n.24, bf16[16,16384]{1,0:T(8,128)(2,1)S(1)} %get-tuple-element.500, ...), kind=kOutput, calls=%fused_computation.19.clone.1 | convolution fusion | flops 72368128 | bytes 224768 | tf_op jit(solution)/shard_map/while/body/eval_jaxpr/dot_general | solution.py:39
  21.6 1.5 %fusion.49 = f32[16,512]{1,0:T(8,128)S(1)} fusion(bf16[16,512]{1,0:T(8,128)(2,1)S(1)} %get-tuple-element.504, f32[2048]{0:T(1024)S(1)} %dynamic_slice.77, f32[512]{0:T(512)S(1)} %get-tuple-element.501, bf16[16,16384]{1,0:T(8,128)(2,1)S(1)} %get-tuple-element.503, s32[]{:T(128)S(6)} %select_n.24, bf16[16,16384]{1,0:T(8,128)(2,1)S(1)} %get-tuple-element.500, ...), kind=kOutput, calls=%fused_computation.19.clone.1 | convolution fusion | flops 72368128 | bytes 224768 | tf_op jit(solution)/shard_map/while/body/eval_jaxpr/dot_general | solution.py:39
  23.1 20.5 %psum.14 = bf16[16,512]{1,0:T(8,128)(2,1)S(1)} all-reduce(bf16[16,512]{1,0:T(8,128)(2,1)S(1)} %convert_element_type.73), channel_id=1, replica_groups=mesh['dp'=2,'ind'=4,'probe'=4] {'ind'}, use_global_device_ids=true, to_apply=%region_4.0 | all-reduce | flops 8192 | bytes 32768 | tf_op jit(solution)/shard_map/psum | solution.py:46
  43.6 0.1 broadcast_in_dim.24
  43.7 0.0 copy-done.1
  43.7 25.0 %while.27 = (s32[]{:T(128)}, f32[16,16384]{1,0:T(8,128)S(1)}, f32[512]{0:T(512)S(1)}, f32[16384]{0:T(1024)S(1)}, bf16[16,16384]{1,0:T(8,128)(2,1)S(1)}, /*index=...) while((s32[]{:T(128)}, f32[16,16384]{1,0:T(8,128)S(1)}, ...), condition=%wide.region_7.0_spmd, body=%wide.region_5.0_spmd.sunk | while | flops 111245312 | bytes 8808643 | solution.py:66
  43.8 1.1 fusion.44
  44.9 0.8 convert_reduce_fusion.2
  45.6 1.2 fusion.45
  46.9 1.1 fusion.44
  48.0 0.8 convert_reduce_fusion.2
  48.8 1.2 fusion.45
  50.0 1.1 fusion.44
  51.1 0.8 convert_reduce_fusion.2
  51.9 1.2 fusion.45
  53.1 1.1 fusion.44
  54.2 0.8 convert_reduce_fusion.2
  55.0 1.2 fusion.45
  56.2 1.1 fusion.44
  57.4 0.8 convert_reduce_fusion.2
  58.1 1.2 fusion.45
  59.4 1.1 fusion.44
  60.5 0.8 convert_reduce_fusion.2
  61.2 1.2 fusion.45
  62.5 1.1 fusion.44
  63.6 0.8 convert_reduce_fusion.2
  64.4 1.2 fusion.45
  65.6 1.1 fusion.44
  66.7 0.8 convert_reduce_fusion.2
  67.5 1.2 fusion.45
  68.7 0.0 copy-start
  68.7 1.0 copy-done
  69.7 0.0 all-reduce.2.cloned.1.call-update
  69.7 55.1 %all-reduce.2.cloned.1.call-done = f32[16,16384]{1,0:T(8,128)} async-done(((f32[16,16384]{1,0:T(8,128)}), f32[16,16384]{1,0:T(8,128)}) %all-reduce.2.cloned.1.call-update) | async-done | bytes 1048592 | tf_op jit(solution)/shard_map/psum | solution.py:69
  124.8 2.3 %broadcast_multiply_fusion = f32[16,16384]{1,0:T(8,128)} fusion(f32[16,16384]{1,0:T(8,128)} %all-reduce.2.cloned.1.call-done, f32[16]{0:T(128)S(1)} %get-tuple-element.358), kind=kLoop, calls=%fused_computation.28 | loop fusion | flops 262144 | bytes 2097216 | tf_op jit(solution)/shard_map/mul | solution.py:71
  (21 shorter events, 0.1 us)
Async XLA Ops:
  6.5 4.7 %copy-start.2 = (bf16[8,16384]{1,0:T(8,128)(2,1)S(1)}, bf16[8,16384]{1,0:T(8,128)(2,1)}, u32[]{:S(2)}) copy-start(bf16[8,16384]{1,0:T(8,128)(2,1)} %param.14) | copy-start | bytes 786436
  6.5 118.3 %all-reduce.2.cloned.1.call-start = ((), (), s32[]{:S(2)}) async-start(), calls=%async_computation | async-start | bytes 2097152 | tf_op jit(solution)/shard_map/psum | solution.py:69
  11.3 32.4 %copy-start.1 = (bf16[16,512]{1,0:T(8,128)(2,1)S(1)}, bf16[16,512]{1,0:T(8,128)(2,1)}, u32[]{:S(2)}) copy-start(bf16[16,512]{1,0:T(8,128)(2,1)} %param.10) | copy-start | bytes 49156
  68.7 1.0 copy-start
Sparse Core Ops, SparseCore 0:
  69.9 54.8 all-reduce.1
where the time goes:
time: 135 us; the launch traced here: 134 us
  waiting for transfers between devices  55.1 us (41%)
  matrix products  36.6 us (27%)
  blocking collectives  20.5 us (15%)
  between operations  14.1 us (10%)
  other arithmetic  6.35 us (5%)
    psum x1, waiting for transfers between devices, on_device(): summed = lax.psum(partial_grad, ('dp', 'probe'))  55.1 us
    psum x1, blocking collectives, on_device(): projections = lax.psum(partial_proj.astype(jnp.bfloat16), 'ind')  20.5 us
    dot_general x8, matrix products, first_pass(): lax.dot_general(stack_part, kern, (((1,), (1,)), ((), ())), preferred_ele...  11.8 us
    dot_general x8, matrix products, second_pass(): moment = jnp.dot(data_x, weighted, preferred_element_type=jnp.float32)  9.92 us
    dot_general x8, matrix products, kernel_block(): lax.dot_general(x_scaled, z_scaled, (((0,), (0,)), ((), ())), preferred_e...  8.83 us
    dot_general x8, matrix products, second_pass(): lax.dot_general(swapped, stack_part, (((0,), (0,)), ((), ())), preferred_...  6.1 us
  transfers between devices with their start and end apart: 1, of which 1 were waited for; matrix products, arithmetic and copies ran while one was open for 0% of the time, Pallas kernels for 0%

commit v1 on v0

v1 whole, which is shorter than its diff:
```python
import functools
import math

import jax
import jax.numpy as jnp
from jax import lax
from jax.experimental import pallas as pl
from jax.experimental.pallas import tpu as pltpu
from jax.sharding import PartitionSpec as P

LOG2E = math.log2(math.e)
F32 = jnp.float32
BF16 = jnp.bfloat16
VMEM = pl.BlockSpec(memory_space=pltpu.VMEM)
SMEM = pl.BlockSpec(memory_space=pltpu.SMEM)
K_ROWS = 64


def tile_of(extent, limit):
    tile = min(extent, limit)
    while extent % tile:
        tile //= 2
    return tile


def column(row):
    d = row.shape[1]
    spread = jnp.broadcast_to(row, (d, d))
    eye = lax.broadcasted_iota(jnp.int32, (d, d), 0) == lax.broadcasted_iota(jnp.int32, (d, d), 1)
    return jnp.sum(jnp.where(eye, spread, 0.0), axis=1, keepdims=True)


def split3(value):
    high = value.astype(BF16).astype(F32)
    rest = value - high
    middle = rest.astype(BF16).astype(F32)
    return high, middle, rest - middle


def padded(parts):
    rows = jnp.concatenate(parts, axis=0)
    return jnp.concatenate([rows, jnp.zeros((K_ROWS - rows.shape[0], rows.shape[1]), F32)], axis=0)


def x_side(x, inverse):
    wide = (x.astype(F32) * inverse).astype(BF16).astype(F32)
    square = jnp.sum(wide * wide, axis=0, keepdims=True) * (-0.5 * LOG2E)
    ones = jnp.ones((3, x.shape[1]), F32)
    return jnp.transpose(padded([*split3(wide * LOG2E), *split3(square), ones])).astype(BF16)


def z_side(z, inverse):
    wide = (z.astype(F32) * inverse).astype(BF16).astype(F32)
    square = jnp.sum(wide * wide, axis=0, keepdims=True) * (-0.5 * LOG2E)
    ones = jnp.ones((3, z.shape[1]), F32)
    return padded([wide, wide, wide, ones, *split3(square)]).astype(BF16)


def kern_body(tile, place_ref, length_ref, x_ref, z_ref, kern_ref):
    inverse = column(1.0 / length_ref[...])
    left = x_side(x_ref[...], inverse)
    columns = kern_ref.shape[1]
    first = place_ref[0] * columns

    def step(index, carry):
        source = pl.ds(pl.multiple_of(first + index * tile, tile), tile)
        target = pl.ds(pl.multiple_of(index * tile, tile), tile)
        right = z_side(z_ref[:, source], inverse)
        kern_ref[:, target] = jnp.exp2(jnp.dot(left, right, preferred_element_type=F32)).astype(BF16)
        return carry

    lax.fori_loop(0, columns // tile, step, 0)


def kern_call(place, length, x, z, columns):
    rows = x.shape[1]
    return pl.pallas_call(
        functools.partial(kern_body, tile_of(columns, 2048)),
        out_shape=pltpu.VMEM((rows, columns), BF16),
        in_specs=[SMEM, VMEM, VMEM, VMEM],
        out_specs=VMEM,
        compiler_params=pltpu.CompilerParams(vmem_limit_bytes=24 << 20),
        cost_estimate=pl.CostEstimate(
            flops=2 * rows * columns * K_ROWS, bytes_accessed=2 * rows * columns, transcendentals=rows * columns
        ),
        name="kern",
    )(place, length, x, z)


def project_body(tile, place_ref, kern_ref, solves_ref, signs_ref, solves2_ref, signs2_ref, stack_ref, own_ref, other_ref):
    columns = kern_ref.shape[1]
    first = place_ref[0] * columns
    total = None
    for index in range(columns // tile):
        source = pl.ds(pl.multiple_of(first + index * tile, tile), tile)
        target = slice(index * tile, (index + 1) * tile)
        part = jnp.concatenate(
            [
                solves_ref[:, source].astype(F32),
                (2 * signs_ref[:, source] - 1).astype(F32),
                solves2_ref[:, source].astype(F32),
                (2 * signs2_ref[:, source] - 1).astype(F32),
            ],
            axis=0,
        ).astype(BF16)
        stack_ref[:, target] = part
        term = lax.dot_general(kern_ref[:, target], part, (((1,), (1,)), ((), ())), preferred_element_type=F32)
        total = term if total is None else total + term
    total = jnp.transpose(total)
    half = total.shape[0] // 2
    own_ref[...] = total[:half]
    other_ref[...] = total[half:].astype(BF16)


def project_call(place, kern, solves, signs, solves2, signs2):
    rows, columns = kern.shape
    probes = solves.shape[0]
    return pl.pallas_call(
        functools.partial(project_body, tile_of(columns, 2048)),
        out_shape=(
            jax.ShapeDtypeStruct((4 * probes, columns), BF16),
            jax.ShapeDtypeStruct((2 * probes, rows), F32),
            jax.ShapeDtypeStruct((2 * probes, rows), BF16),
        ),
        in_specs=[SMEM] + [VMEM] * 5,
        out_specs=(VMEM,) * 3,
        compiler_params=pltpu.CompilerParams(vmem_limit_bytes=24 << 20),
        cost_estimate=pl.CostEstimate(
            flops=8 * rows * columns * probes, bytes_accessed=2 * rows * columns, transcendentals=0
        ),
        name="project",
    )(place, kern, solves, signs, solves2, signs2)


def gradient_body(
    tile, groups, halves, p_size, place_ref, noise_ref, length_ref, z_ref, stacks, projections, data, kerns, grad_ref
):
    core, group = place_ref[0], place_ref[1]
    columns = grad_ref.shape[1]
    first = core * columns
    inverse = column(1.0 / length_ref[...])
    factor = inverse * inverse / (noise_ref[0] * p_size)

    def in_order(values):
        if groups != 2:
            return values
        own, other = values
        return [jnp.where(group == 0, own, other), jnp.where(group == 0, other, own)]

    lefts, rows = [], []
    for half in range(halves):
        blocks = []
        for index in range(groups):
            parts = []
            for block in (projections[0], projections[1]):
                value = block[half * groups + index].astype(F32)
                middle = value.shape[0] // 2
                parts += [value[middle:], value[:middle]]
            blocks.append(jnp.concatenate(parts, axis=0))
        lefts.append(jnp.transpose(jnp.concatenate(in_order(blocks), axis=0)).astype(BF16))
        x = data[half][...].astype(F32)
        rows.append(jnp.concatenate([x, jnp.ones((16, x.shape[1]), F32)], axis=0).astype(BF16))
    dims = data[0].shape[0]

    def step(index, carry):
        source = pl.ds(pl.multiple_of(first + index * tile, tile), tile)
        target = pl.ds(pl.multiple_of(index * tile, tile), tile)
        stack = jnp.concatenate(in_order([ref[:, target].astype(F32) for ref in stacks]), axis=0).astype(BF16)
        total = None
        for half in range(halves):
            coef = jnp.dot(lefts[half], stack, preferred_element_type=F32)
            weighted = (kerns[half][:, target].astype(F32) * coef).astype(BF16)
            term = jnp.dot(rows[half], weighted, preferred_element_type=F32)
            total = term if total is None else total + term
        z = z_ref[:, source].astype(F32)
        grad_ref[:, target] = ((total[:dims] - z * total[dims : dims + 1]) * factor).astype(grad_ref.dtype)
        return carry

    lax.fori_loop(0, columns // tile, step, 0)


def gradient_call(place, noise, length, z, stacks, projections, data, kerns, p_size, dtype):
    rows, columns = kerns[0].shape
    groups, halves = len(stacks), len(kerns)

    def body(place_ref, noise_ref, length_ref, z_ref, *refs):
        refs = list(refs)
        take = lambda count: [refs.pop(0) for _ in range(count)]
        stack_refs, projection_refs, data_refs, kern_refs = take(groups), take(2), take(halves), take(halves)
        gradient_body(
            tile_of(columns, 1024), groups, halves, p_size, place_ref, noise_ref, length_ref, z_ref,
            stack_refs, projection_refs, data_refs, kern_refs, refs[0],
        )

    return pl.pallas_call(
        body,
        out_shape=jax.ShapeDtypeStruct((z.shape[0], columns), dtype),
        in_specs=[SMEM, SMEM] + [VMEM] * (2 + groups + 2 + 2 * halves),
        out_specs=VMEM,
        compiler_params=pltpu.CompilerParams(vmem_limit_bytes=32 << 20),
        cost_estimate=pl.CostEstimate(
            flops=2 * halves * rows * columns * 128, bytes_accessed=2 * halves * rows * columns, transcendentals=0
        ),
        name="gradient",
    )(place, noise, length, z, *stacks, *projections, *data, *kerns)


def solution(mesh):
    dp, ind, probe = mesh.shape["dp"], mesh.shape["ind"], mesh.shape["probe"]
    groups = probe // 2
    halves = dp if dp <= 2 else 1
    core_swap = [(i, i ^ 1) for i in range(probe)]

    def cores(value):
        return lax.ppermute(value, "probe", core_swap)

    def from_group(shift):
        return [((i + 2 * shift) % probe, i) for i in range(probe)]

    def on_device(data_x, inducing_z, lengthscale, noise_var, solves, probe_signs):
        columns = inducing_z.shape[1] // 2
        p_size = solves.shape[0] * probe
        place_index = lax.axis_index("probe")
        place = jnp.stack([place_index % 2, place_index // 2]).astype(jnp.int32)
        length = lengthscale.reshape(1, -1)

        solves2, signs2 = cores(solves), cores(probe_signs)
        data = [data_x] + [lax.ppermute(data_x, "dp", [(i, 1 - i) for i in range(dp)]) for _ in range(halves - 1)]
        kerns = [kern_call(place, length, data_x, inducing_z, columns)]
        stack, own, other = project_call(place, kerns[0], solves, probe_signs, solves2, signs2)
        stacks = [stack] + [lax.ppermute(stack, "probe", from_group(s)) for s in range(1, groups)]
        kerns += [kern_call(place, length, x, inducing_z, columns) for x in data[1:]]

        part = (own + cores(other).astype(F32)).astype(BF16)
        peers = [lax.ppermute(part, "ind", [((i ^ s), i) for i in range(ind)]) for s in range(1, ind)]
        block = sum([p.astype(F32) for p in peers], part.astype(F32)).astype(BF16)

        blocks = []
        for half in range(halves):
            for shift in range(groups):
                pairs = []
                for d in range(dp):
                    for source, target in from_group(shift):
                        pairs.append(((d ^ half) * probe + source, d * probe + target))
                blocks.append(block if half == 0 and shift == 0 else lax.ppermute(block, ("dp", "probe"), pairs))
        own_blocks = jnp.stack(blocks)
        other_blocks = cores(own_blocks)

        whole = halves == dp
        grad = gradient_call(
            place, noise_var, length, inducing_z, stacks, (own_blocks, other_blocks), data, kerns, p_size,
            BF16 if whole else F32,
        )
        if not whole:
            grad = lax.psum(grad, "dp").astype(BF16)
        far = cores(grad)
        lower = place[0] == 0
        return jnp.concatenate(
            [jnp.where(lower, grad, far).astype(F32), jnp.where(lower, far, grad).astype(F32)], axis=1
        )

    return jax.shard_map(
        on_device,
        mesh=mesh,
        in_specs=(P(None, "dp"), P(None, "ind"), P(), P(), P("probe", "ind"), P("probe", "ind")),
        out_specs=P(None, "ind"),
        check_vma=False,
    )
```

time: 135 us -> 43.8 us (0.32)
  waiting for transfers between devices: 55.1 us -> 6.61 us
  matrix products: 36.6 us -> 0 us
  blocking collectives: 20.5 us -> 0 us
  Pallas kernels: 0 us -> 19 us
  starting transfers between devices: 0.01 us -> 13.6 us
  between operations: 14.1 us -> 0.79 us
  other arithmetic: 6.35 us -> 1.18 us
    psum x1 -> x0, waiting for transfers between devices: 55.1 us -> none  [on_device(): summed = lax.psum(partial_grad, ('dp', 'probe'))]
    dot_general x32 -> x0, matrix products: 36.6 us -> none  [the longest x8 11.8 us: first_pass(): lax.dot_general(stack_part, kern, (((1,), (1,)), ((), ())), preferred_ele...]
    psum x1 -> x0, blocking collectives: 20.5 us -> none  [on_device(): projections = lax.psum(partial_proj.astype(jnp.bfloat16), 'ind')]
    pallas_call x0 -> x4, Pallas kernels: none -> 19 us  [the longest x1 8.99 us: gradient_call(): pl.pallas_call(body, out_shape=jax.ShapeDtypeStruct((z.shape[0], columns)...]
    ppermute x0 -> x13, starting transfers between devices: none -> 13.6 us  [the longest x3 4.45 us: on_device(): lax.ppermute(part, 'ind', [(i ^ s, i) for i in range(ind)])]
    ppermute x0 -> x13, waiting for transfers between devices: none -> 6.61 us  [the longest x3 3.85 us: on_device(): lax.ppermute(part, 'ind', [(i ^ s, i) for i in range(ind)])]
    mul x1 -> x0, other arithmetic: 2.33 us -> none  [on_device(): return summed * factor[:, None]]
    reduce_sum x2 -> x0, other arithmetic: 2.19 us -> none  [the longest x1 1.39 us: on_device(): z_square = jnp.sum(z_wide * z_wide, axis=0)]
  transfers between devices with their start and end apart: 1 -> 13, of which waited for: 1 -> 6; matrix products, arithmetic and copies ran while one was open for 0% -> 0% of each run, Pallas kernels for 0% -> 16%
where the time goes in v1:
time: 43.8 us; the launch traced here: 43.5 us
  Pallas kernels  19 us (43%)
  starting transfers between devices  13.6 us (31%)
  waiting for transfers between devices  6.61 us (15%)
  local copies, waits for them, and re-layouts  2.44 us (6%)
  other arithmetic  1.18 us (3%)
  between operations  0.79 us (2%)
    pallas_call x1, Pallas kernels, gradient_call(): pl.pallas_call(body, out_shape=jax.ShapeDtypeStruct((z.shape[0], columns)...  8.99 us
    pallas_call x2, Pallas kernels, kern_call(): pl.pallas_call(functools.partial(kern_body, tile_of(columns, 2048)), out_...  7.06 us
    ppermute x3, starting transfers between devices, on_device(): lax.ppermute(part, 'ind', [(i ^ s, i) for i in range(ind)])  4.45 us
    ppermute x3, waiting for transfers between devices, on_device(): lax.ppermute(part, 'ind', [(i ^ s, i) for i in range(ind)])  3.85 us
    ppermute x3, starting transfers between devices, on_device(): lax.ppermute(block, ('dp', 'probe'), pairs)  3.55 us
    pallas_call x1, Pallas kernels, project_call(): pl.pallas_call(functools.partial(project_body, tile_of(columns, 2048)), o...  2.9 us
    ppermute x1, starting transfers between devices, on_device(): lax.ppermute(stack, 'probe', from_group(s))  2.59 us
    unnamed x16, local copies, waits for them, and re-layouts  2.44 us
  transfers between devices with their start and end apart: 13, of which 6 were waited for; matrix products, arithmetic and copies ran while one was open for 0% of the time, Pallas kernels for 16%

profile of v1, /device:TPU:0, one launch (start us, length us, event | category | flops | bytes accessed | tf_op | source)
XLA Modules:
  0.0 43.5 jit_solution(7746234671079088125)
XLA Ops:
  0.0 0.5 %collective-permute-start.1 = (s32[8,16384]{1,0:T(8,128)}, s32[8,16384]{1,0:T(8,128)S(1)}, u32[]{:S(2)}, u32[]{:S(2)}) collective-permute-start(s32[8,16384]{1,0:T(8,128)} %signs_ref.1), channel_id=1, source_target_pairs={{0,1},{1,0},{2,3},{3,2},{4,5},{5,4},{6,7},{7,6},{8,9},{9,8},{10,11... | collective-permute-start | bytes 1572872 | tf_op jit(solution)/shard_map/ppermute | solution.py:215
  0.5 0.0 collective-permute-start
  0.5 0.1 pad_add_fusion.place_ref
  0.6 0.0 copy-start
  0.6 1.0 %copy-done = bf16[16,16384]{1,0:T(8,128)(2,1)S(1)} copy-done((bf16[16,16384]{1,0:T(8,128)(2,1)S(1)}, bf16[16,16384]{1,0:T(8,128)(2,1)}, u32[]{:S(2)}) %copy-start) | copy-done | bytes 524312
  1.6 0.0 copy-start.4
  1.6 0.7 %copy-done.4 = bf16[16,512]{1,0:T(8,128)(2,1)S(1)} copy-done((bf16[16,512]{1,0:T(8,128)(2,1)S(1)}, bf16[16,512]{1,0:T(8,128)(2,1)}, u32[]{:S(2)}) %copy-start.4) | copy-done | bytes 16408
  2.3 0.0 copy-start.6
  2.3 0.7 %copy-done.6 = f32[16]{0:T(128)S(1)} copy-done((f32[16]{0:T(128)S(1)}, f32[16]{0:T(128)}, u32[]{:S(2)}) %copy-start.6) | copy-done | bytes 88
  3.0 0.0 copy-start.2
  3.0 0.0 copy-start.3
  3.0 0.0 copy-start.1
  3.0 3.5 %kern.2.kern_ref.refs_6_ = bf16[512,8192]{1,0:T(8,128)(2,1)S(1)} custom-call(s32[2]{0:T(128)S(1)} %pad_add_fusion.place_ref, f32[1,16]{1,0:T(1,128)S(1)} %bitcast.7, bf16[16,512]{1,0:T(8,128)(2,1)S(1)} %copy-done.4, bf16[16,16384]{1,0:T(8,128)(2,1)S(1)} %copy-done), custom_call_target="tpu_custom_call" | custom-call | flops 536870912 | bytes 8388608 | tf_op jit(solution)/shard_map/kern/pallas_call | solution.py:77
  6.5 0.0 copy-start.5
  6.6 0.0 copy-start.7
  6.6 0.0 collective-permute-done.solves2_ref
  6.6 0.0 collective-permute-done.1.signs2_ref
  6.6 0.0 copy-done.2
  6.6 0.0 copy-done.3
  6.6 2.9 %project.1 = (bf16[32,8192]{1,0:T(8,128)(2,1)S(1)}, f32[16,512]{1,0:T(8,128)S(1)}, bf16[16,512]{1,0:T(8,128)(2,1)S(1)}) custom-call(s32[2]{0:T(128)S(1)} %pad_add_fusion.place_ref, bf16[512,8192]{1,0:T(8,128)(2,1)S(1)} %kern.2.kern_ref.refs_6_, bf16[8,16384]{1,0:T(8,128)(2,1)S(1)} %copy-done.3, s32[8,16384]{1,0:T(8,128)S(1)} %copy-done.2, ...), custom_call_target="tpu_custom_call" | custom-call | flops 268435456 | bytes 8388608 | tf_op jit(solution)/shard_map/project/pallas_call | solution.py:118
  9.5 0.5 %collective-permute-start.3 = (bf16[16,512]{1,0:T(8,128)(2,1)S(1)}, bf16[16,512]{1,0:T(8,128)(2,1)S(1)}, u32[]{:S(2)}, u32[]{:S(2)}) collective-permute-start(bf16[16,512]{1,0:T(8,128)(2,1)S(1)} %get-tuple-element.10), channel_id=1, source_target_pairs={{0,1},{1,0},{2,3},{3,2},{4,5},{5,4},{6,7},{7,6},{8,9},{9,8},{10,11... | collective-permute-start | bytes 49160 | tf_op jit(solution)/shard_map/ppermute | solution.py:215
  10.0 2.6 %collective-permute-start.2 = (bf16[32,8192]{1,0:T(8,128)(2,1)S(1)}, bf16[32,8192]{1,0:T(8,128)(2,1)S(1)}, u32[]{:S(2)}, u32[]{:S(2)}) collective-permute-start(bf16[32,8192]{1,0:T(8,128)(2,1)S(1)} %get-tuple-element.8.refs_0_), channel_id=1, source_target_pairs={{2,0},{3,1},{0,2},{1,3},{6,4},{7,5},{4,6},{5,7},{10,8},{11,9},{8,1... | collective-permute-start | bytes 1572872 | tf_op jit(solution)/shard_map/ppermute | solution.py:231
  12.6 0.0 collective-permute-done.3
  12.6 3.7 %collective-permute-start.6 = (bf16[16,512]{1,0:T(8,128)(2,1)S(1)}, bf16[16,512]{1,0:T(8,128)(2,1)S(1)}, u32[]{:S(2)}, u32[]{:S(2)}) collective-permute-start(bf16[16,512]{1,0:T(8,128)(2,1)S(1)} %add_convert_fusion.1), channel_id=1, source_target_pairs={{12,0},{8,4},{4,8},{0,12},{13,1},{9,5},{5,9},{1,13},{14,2},{10,6},... | collective-permute-start | bytes 49160 | tf_op jit(solution)/shard_map/ppermute | solution.py:235
  16.3 0.0 collective-permute-start.5
  16.3 0.8 %collective-permute-start.4 = (bf16[16,512]{1,0:T(8,128)(2,1)S(1)}, bf16[16,512]{1,0:T(8,128)(2,1)S(1)}, u32[]{:S(2)}, u32[]{:S(2)}) collective-permute-start(bf16[16,512]{1,0:T(8,128)(2,1)S(1)} %add_convert_fusion.1), channel_id=1, source_target_pairs={{4,0},{0,4},{12,8},{8,12},{5,1},{1,5},{13,9},{9,13},{6,2},{2,6},{1... | collective-permute-start | bytes 49160 | tf_op jit(solution)/shard_map/ppermute | solution.py:235
  17.1 1.1 %collective-permute-done.6 = bf16[16,512]{1,0:T(8,128)(2,1)S(1)} collective-permute-done((bf16[16,512]{1,0:T(8,128)(2,1)S(1)}, bf16[16,512]{1,0:T(8,128)(2,1)S(1)}, u32[]{:S(2)}, u32[]{:S(2)}) %collective-permute-start.6) | collective-permute-done | bytes 16416 | tf_op jit(solution)/shard_map/ppermute | solution.py:235
  18.3 2.7 %collective-permute-done.5 = bf16[16,512]{1,0:T(8,128)(2,1)S(1)} collective-permute-done((bf16[16,512]{1,0:T(8,128)(2,1)S(1)}, bf16[16,512]{1,0:T(8,128)(2,1)S(1)}, u32[]{:S(2)}, u32[]{:S(2)}) %collective-permute-start.5) | collective-permute-done | bytes 16416 | tf_op jit(solution)/shard_map/ppermute | solution.py:235
  20.9 0.0 collective-permute-done.4
  21.0 2.0 %collective-permute-start.9 = (bf16[16,512]{1,0:T(8,128)(2,1)S(1)}, bf16[16,512]{1,0:T(8,128)(2,1)S(1)}, u32[]{:S(2)}, u32[]{:S(2)}) collective-permute-start(bf16[16,512]{1,0:T(8,128)(2,1)S(1)} %add_convert_fusion), channel_id=1, source_target_pairs={{18,0},{19,1},{16,2},{17,3},{2,16},{3,17},{0,18},{1,19},{22,4},{23... | collective-permute-start | bytes 49160 | tf_op jit(solution)/shard_map/ppermute | solution.py:245
  23.0 0.5 %collective-permute-start.8 = (bf16[16,512]{1,0:T(8,128)(2,1)S(1)}, bf16[16,512]{1,0:T(8,128)(2,1)S(1)}, u32[]{:S(2)}, u32[]{:S(2)}) collective-permute-start(bf16[16,512]{1,0:T(8,128)(2,1)S(1)} %add_convert_fusion), channel_id=1, source_target_pairs={{16,0},{17,1},{18,2},{19,3},{0,16},{1,17},{2,18},{3,19},{20,4},{21... | collective-permute-start | bytes 49160 | tf_op jit(solution)/shard_map/ppermute | solution.py:245
  23.5 1.0 %collective-permute-start.7 = (bf16[16,512]{1,0:T(8,128)(2,1)S(1)}, bf16[16,512]{1,0:T(8,128)(2,1)S(1)}, u32[]{:S(2)}, u32[]{:S(2)}) collective-permute-start(bf16[16,512]{1,0:T(8,128)(2,1)S(1)} %add_convert_fusion), channel_id=1, source_target_pairs={{2,0},{3,1},{0,2},{1,3},{18,16},{19,17},{16,18},{17,19},{6,4},{7,5... | collective-permute-start | bytes 49160 | tf_op jit(solution)/shard_map/ppermute | solution.py:245
  24.5 1.5 %collective-permute-start.11 = (bf16[16,512]{1,0:T(8,128)(2,1)S(1)}, bf16[16,512]{1,0:T(8,128)(2,1)S(1)}, u32[]{:S(2)}, u32[]{:S(2)}) collective-permute-start(bf16[16,512]{1,0:T(8,128)(2,1)S(1)} %copy-done.4), channel_id=1, source_target_pairs={{0,16},{16,0},{1,17},{17,1},{2,18},{18,2},{3,19},{19,3},{4,20},{20... | collective-permute-start | bytes 49160 | tf_op jit(solution)/shard_map/ppermute | solution.py:228
  26.0 0.0 collective-permute-done.9
  26.0 0.7 %collective-permute-done.8 = bf16[16,512]{1,0:T(8,128)(2,1)S(1)} collective-permute-done((bf16[16,512]{1,0:T(8,128)(2,1)S(1)}, bf16[16,512]{1,0:T(8,128)(2,1)S(1)}, u32[]{:S(2)}, u32[]{:S(2)}) %collective-permute-start.8) | collective-permute-done | bytes 16416 | tf_op jit(solution)/shard_map/ppermute | solution.py:245
  26.8 0.5 %collective-permute-done.7 = bf16[16,512]{1,0:T(8,128)(2,1)S(1)} collective-permute-done((bf16[16,512]{1,0:T(8,128)(2,1)S(1)}, bf16[16,512]{1,0:T(8,128)(2,1)S(1)}, u32[]{:S(2)}, u32[]{:S(2)}) %collective-permute-start.7) | collective-permute-done | bytes 16416 | tf_op jit(solution)/shard_map/ppermute | solution.py:245
  27.3 0.1 collective-permute-start.10
  28.0 0.2 collective-permute-done.11.x_ref.refs_5_
  28.3 0.0 copy-done.1
  28.3 3.5 %kern.3.refs_7_ = bf16[512,8192]{1,0:T(8,128)(2,1)S(1)} custom-call(s32[2]{0:T(128)S(1)} %pad_add_fusion.place_ref, f32[1,16]{1,0:T(1,128)S(1)} %bitcast.8, bf16[16,512]{1,0:T(8,128)(2,1)S(1)} %collective-permute-done.11.x_ref.refs_5_, bf16[16,16384]{1,0:T(8,128)(2,1)S(1)} %copy-done.1), custom_call_target="tpu_custom_call" | custom-call | flops 536870912 | bytes 8388608 | tf_op jit(solution)/shard_map/kern/pallas_call | solution.py:77
  31.8 0.0 collective-permute-done.10.refs_3_
  31.8 0.0 collective-permute-done.2.refs_1_
  31.8 0.0 copy-done.5
  31.8 0.0 copy-done.7
  31.8 9.0 %gradient.1 = bf16[16,8192]{1,0:T(8,128)(2,1)S(1)} custom-call(s32[2]{0:T(128)S(1)} %pad_add_fusion.place_ref, f32[1]{0:T(128)S(6)} %copy.7.noise_ref, f32[1,16]{1,0:T(1,128)S(1)} %bitcast.9, bf16[16,16384]{1,0:T(8,128)(2,1)S(1)} %copy-done.1, bf16[32,8192]{1,0:T(8,128)(2,1)S(1)} %get-tuple-element.8.refs_0_, ...), custom_call_target="tpu_custom_call" | custom-call | flops 2147483648 | bytes 16777216 | tf_op jit(solution)/shard_map/gradient/pallas_call | solution.py:195
  40.8 0.3 collective-permute-start.12
  41.2 1.3 %collective-permute-done.12 = bf16[16,8192]{1,0:T(8,128)(2,1)S(1)} collective-permute-done((bf16[16,8192]{1,0:T(8,128)(2,1)S(1)}, bf16[16,8192]{1,0:T(8,128)(2,1)S(1)}, u32[]{:S(2)}, u32[]{:S(2)}) %collective-permute-start.12) | collective-permute-done | bytes 262176 | tf_op jit(solution)/shard_map/ppermute | solution.py:215
  42.5 1.0 %maximum_convert_fusion = f32[16,16384]{1,0:T(8,128)} fusion(bf16[16,8192]{1,0:T(8,128)(2,1)S(1)} %get-tuple-element.12, bf16[16,8192]{1,0:T(8,128)(2,1)S(1)} %get-tuple-element.11), kind=kLoop, calls=%fused_computation | loop fusion | flops 1048576 | bytes 1572864 | tf_op jit(solution)/shard_map/concatenate | solution.py:258
  (4 shorter events, 0.1 us)
Async XLA Ops:
  0.0 6.6 %collective-permute-start.1 = (s32[8,16384]{1,0:T(8,128)}, s32[8,16384]{1,0:T(8,128)S(1)}, u32[]{:S(2)}, u32[]{:S(2)}) collective-permute-start(s32[8,16384]{1,0:T(8,128)} %signs_ref.1), channel_id=1, source_target_pairs={{0,1},{1,0},{2,3},{3,2},{4,5},{5,4},{6,7},{7,6},{8,9},{9,8},{10,11... | collective-permute-start | bytes 1572872 | tf_op jit(solution)/shard_map/ppermute | solution.py:215
  0.5 6.1 %collective-permute-start = (bf16[8,16384]{1,0:T(8,128)(2,1)}, bf16[8,16384]{1,0:T(8,128)(2,1)S(1)}, u32[]{:S(2)}, u32[]{:S(2)}) collective-permute-start(bf16[8,16384]{1,0:T(8,128)(2,1)} %solves_ref.1), channel_id=1, source_target_pairs={{0,1},{1,0},{2,3},{3,2},{4,5},{5,4},{6,7},{7,6},{8,9},{9,8},{10,11... | collective-permute-start | bytes 786440 | tf_op jit(solution)/shard_map/ppermute | solution.py:215
  0.6 1.0 %copy-start = (bf16[16,16384]{1,0:T(8,128)(2,1)S(1)}, bf16[16,16384]{1,0:T(8,128)(2,1)}, u32[]{:S(2)}) copy-start(bf16[16,16384]{1,0:T(8,128)(2,1)} %z_ref.5) | copy-start | bytes 1572868
  1.6 0.7 %copy-start.4 = (bf16[16,512]{1,0:T(8,128)(2,1)S(1)}, bf16[16,512]{1,0:T(8,128)(2,1)}, u32[]{:S(2)}) copy-start(bf16[16,512]{1,0:T(8,128)(2,1)} %refs_4_.1) | copy-start | bytes 49156
  2.3 0.7 %copy-start.6 = (f32[16]{0:T(128)S(1)}, f32[16]{0:T(128)}, u32[]{:S(2)}) copy-start(f32[16]{0:T(128)} %param.8) | copy-start | bytes 196
  3.0 3.6 %copy-start.2 = (s32[8,16384]{1,0:T(8,128)S(1)}, s32[8,16384]{1,0:T(8,128)}, u32[]{:S(2)}) copy-start(s32[8,16384]{1,0:T(8,128)} %signs_ref.1) | copy-start | bytes 1572868
  3.0 3.6 %copy-start.3 = (bf16[8,16384]{1,0:T(8,128)(2,1)S(1)}, bf16[8,16384]{1,0:T(8,128)(2,1)}, u32[]{:S(2)}) copy-start(bf16[8,16384]{1,0:T(8,128)(2,1)} %solves_ref.1) | copy-start | bytes 786436
  3.0 25.3 %copy-start.1 = (bf16[16,16384]{1,0:T(8,128)(2,1)S(1)}, bf16[16,16384]{1,0:T(8,128)(2,1)}, u32[]{:S(2)}) copy-start(bf16[16,16384]{1,0:T(8,128)(2,1)} %z_ref.5) | copy-start | bytes 1572868
  6.5 25.3 %copy-start.5 = (bf16[16,512]{1,0:T(8,128)(2,1)S(1)}, bf16[16,512]{1,0:T(8,128)(2,1)}, u32[]{:S(2)}) copy-start(bf16[16,512]{1,0:T(8,128)(2,1)} %refs_4_.1) | copy-start | bytes 49156
  6.6 25.3 %copy-start.7 = (f32[16]{0:T(128)S(1)}, f32[16]{0:T(128)}, u32[]{:S(2)}) copy-start(f32[16]{0:T(128)} %param.8) | copy-start | bytes 196
  9.5 3.1 %collective-permute-start.3 = (bf16[16,512]{1,0:T(8,128)(2,1)S(1)}, bf16[16,512]{1,0:T(8,128)(2,1)S(1)}, u32[]{:S(2)}, u32[]{:S(2)}) collective-permute-start(bf16[16,512]{1,0:T(8,128)(2,1)S(1)} %get-tuple-element.10), channel_id=1, source_target_pairs={{0,1},{1,0},{2,3},{3,2},{4,5},{5,4},{6,7},{7,6},{8,9},{9,8},{10,11... | collective-permute-start | bytes 49160 | tf_op jit(solution)/shard_map/ppermute | solution.py:215
  10.0 21.8 %collective-permute-start.2 = (bf16[32,8192]{1,0:T(8,128)(2,1)S(1)}, bf16[32,8192]{1,0:T(8,128)(2,1)S(1)}, u32[]{:S(2)}, u32[]{:S(2)}) collective-permute-start(bf16[32,8192]{1,0:T(8,128)(2,1)S(1)} %get-tuple-element.8.refs_0_), channel_id=1, source_target_pairs={{2,0},{3,1},{0,2},{1,3},{6,4},{7,5},{4,6},{5,7},{10,8},{11,9},{8,1... | collective-permute-start | bytes 1572872 | tf_op jit(solution)/shard_map/ppermute | solution.py:231
  12.6 5.6 %collective-permute-start.6 = (bf16[16,512]{1,0:T(8,128)(2,1)S(1)}, bf16[16,512]{1,0:T(8,128)(2,1)S(1)}, u32[]{:S(2)}, u32[]{:S(2)}) collective-permute-start(bf16[16,512]{1,0:T(8,128)(2,1)S(1)} %add_convert_fusion.1), channel_id=1, source_target_pairs={{12,0},{8,4},{4,8},{0,12},{13,1},{9,5},{5,9},{1,13},{14,2},{10,6},... | collective-permute-start | bytes 49160 | tf_op jit(solution)/shard_map/ppermute | solution.py:235
  16.3 4.6 %collective-permute-start.5 = (bf16[16,512]{1,0:T(8,128)(2,1)S(1)}, bf16[16,512]{1,0:T(8,128)(2,1)S(1)}, u32[]{:S(2)}, u32[]{:S(2)}) collective-permute-start(bf16[16,512]{1,0:T(8,128)(2,1)S(1)} %add_convert_fusion.1), channel_id=1, source_target_pairs={{8,0},{12,4},{0,8},{4,12},{9,1},{13,5},{1,9},{5,13},{10,2},{14,6},... | collective-permute-start | bytes 49160 | tf_op jit(solution)/shard_map/ppermute | solution.py:235
  16.3 4.6 %collective-permute-start.4 = (bf16[16,512]{1,0:T(8,128)(2,1)S(1)}, bf16[16,512]{1,0:T(8,128)(2,1)S(1)}, u32[]{:S(2)}, u32[]{:S(2)}) collective-permute-start(bf16[16,512]{1,0:T(8,128)(2,1)S(1)} %add_convert_fusion.1), channel_id=1, source_target_pairs={{4,0},{0,4},{12,8},{8,12},{5,1},{1,5},{13,9},{9,13},{6,2},{2,6},{1... | collective-permute-start | bytes 49160 | tf_op jit(solution)/shard_map/ppermute | solution.py:235
  21.0 5.1 %collective-permute-start.9 = (bf16[16,512]{1,0:T(8,128)(2,1)S(1)}, bf16[16,512]{1,0:T(8,128)(2,1)S(1)}, u32[]{:S(2)}, u32[]{:S(2)}) collective-permute-start(bf16[16,512]{1,0:T(8,128)(2,1)S(1)} %add_convert_fusion), channel_id=1, source_target_pairs={{18,0},{19,1},{16,2},{17,3},{2,16},{3,17},{0,18},{1,19},{22,4},{23... | collective-permute-start | bytes 49160 | tf_op jit(solution)/shard_map/ppermute | solution.py:245
  23.0 3.7 %collective-permute-start.8 = (bf16[16,512]{1,0:T(8,128)(2,1)S(1)}, bf16[16,512]{1,0:T(8,128)(2,1)S(1)}, u32[]{:S(2)}, u32[]{:S(2)}) collective-permute-start(bf16[16,512]{1,0:T(8,128)(2,1)S(1)} %add_convert_fusion), channel_id=1, source_target_pairs={{16,0},{17,1},{18,2},{19,3},{0,16},{1,17},{2,18},{3,19},{20,4},{21... | collective-permute-start | bytes 49160 | tf_op jit(solution)/shard_map/ppermute | solution.py:245
  23.5 3.7 %collective-permute-start.7 = (bf16[16,512]{1,0:T(8,128)(2,1)S(1)}, bf16[16,512]{1,0:T(8,128)(2,1)S(1)}, u32[]{:S(2)}, u32[]{:S(2)}) collective-permute-start(bf16[16,512]{1,0:T(8,128)(2,1)S(1)} %add_convert_fusion), channel_id=1, source_target_pairs={{2,0},{3,1},{0,2},{1,3},{18,16},{19,17},{16,18},{17,19},{6,4},{7,5... | collective-permute-start | bytes 49160 | tf_op jit(solution)/shard_map/ppermute | solution.py:245
  24.5 3.7 %collective-permute-start.11 = (bf16[16,512]{1,0:T(8,128)(2,1)S(1)}, bf16[16,512]{1,0:T(8,128)(2,1)S(1)}, u32[]{:S(2)}, u32[]{:S(2)}) collective-permute-start(bf16[16,512]{1,0:T(8,128)(2,1)S(1)} %copy-done.4), channel_id=1, source_target_pairs={{0,16},{16,0},{1,17},{17,1},{2,18},{18,2},{3,19},{19,3},{4,20},{20... | collective-permute-start | bytes 49160 | tf_op jit(solution)/shard_map/ppermute | solution.py:228
  27.3 4.5 %collective-permute-start.10 = (bf16[4,16,512]{2,1,0:T(8,128)(2,1)S(1)}, bf16[4,16,512]{2,1,0:T(8,128)(2,1)S(1)}, u32[]{:S(2)}, u32[]{:S(2)}) collective-permute-start(bf16[4,16,512]{2,1,0:T(8,128)(2,1)S(1)} %pad_maximum_fusion.refs_2_), channel_id=1, source_target_pairs={{0,1},{1,0},{2,3},{3,2},{4,5},{5,4},{6,7},{7,6},{8,9},{9,8},{10,11... | collective-permute-start | bytes 196616 | tf_op jit(solution)/shard_map/ppermute | solution.py:215
  40.8 1.6 %collective-permute-start.12 = (bf16[16,8192]{1,0:T(8,128)(2,1)S(1)}, bf16[16,8192]{1,0:T(8,128)(2,1)S(1)}, u32[]{:S(2)}, u32[]{:S(2)}) collective-permute-start(bf16[16,8192]{1,0:T(8,128)(2,1)S(1)} %gradient.1), channel_id=1, source_target_pairs={{0,1},{1,0},{2,3},{3,2},{4,5},{5,4},{6,7},{7,6},{8,9},{9,8},{10,11... | collective-permute-start | bytes 786440 | tf_op jit(solution)/shard_map/ppermute | solution.py:215

commit v2 on v1

v2 whole, which is shorter than its diff:
```python
import functools
import math

import jax
import jax.numpy as jnp
from jax import lax
from jax.experimental import pallas as pl
from jax.experimental.pallas import tpu as pltpu
from jax.sharding import PartitionSpec as P

LOG2E = math.log2(math.e)
F32 = jnp.float32
BF16 = jnp.bfloat16
VMEM = pl.BlockSpec(memory_space=pltpu.VMEM)
HBM = pl.BlockSpec(memory_space=pltpu.HBM)
SMEM = pl.BlockSpec(memory_space=pltpu.SMEM)
K_ROWS = 128


def tile_of(extent, limit):
    tile = min(extent, limit)
    while extent % tile:
        tile //= 2
    return tile


def column(row):
    d = row.shape[1]
    spread = jnp.broadcast_to(row, (d, d))
    eye = lax.broadcasted_iota(jnp.int32, (d, d), 0) == lax.broadcasted_iota(jnp.int32, (d, d), 1)
    return jnp.sum(jnp.where(eye, spread, 0.0), axis=1, keepdims=True)


def split3(value):
    high = value.astype(BF16).astype(F32)
    rest = value - high
    middle = rest.astype(BF16).astype(F32)
    return high, middle, rest - middle


def padded(parts):
    rows = jnp.concatenate(parts, axis=0)
    return jnp.concatenate([rows, jnp.zeros((K_ROWS - rows.shape[0], rows.shape[1]), F32)], axis=0)


def x_side(x, inverse):
    wide = (x.astype(F32) * inverse).astype(BF16).astype(F32)
    square = jnp.sum(wide * wide, axis=0, keepdims=True) * (-0.5 * LOG2E)
    ones = jnp.ones((3, x.shape[1]), F32)
    return jnp.transpose(padded([*split3(wide * LOG2E), *split3(square), ones])).astype(BF16)


def z_side(z, inverse):
    wide = (z.astype(F32) * inverse).astype(BF16).astype(F32)
    square = jnp.sum(wide * wide, axis=0, keepdims=True) * (-0.5 * LOG2E)
    ones = jnp.ones((3, z.shape[1]), F32)
    return padded([wide, wide, wide, ones, *split3(square)]).astype(BF16)


def stacked(solves, signs):
    return jnp.concatenate([solves.astype(F32), (2 * signs - 1).astype(F32)], axis=0).astype(BF16)


def kern_tiles(tile, inverse, x, z_ref, kern_ref, arrived):
    left = x_side(x, inverse)
    for index in range(kern_ref.shape[1] // tile):
        arrived(index)
        target = slice(index * tile, (index + 1) * tile)
        right = z_side(z_ref[:, target], inverse)
        kern_ref[:, target] = jnp.exp2(jnp.dot(left, right, preferred_element_type=F32)).astype(BF16)


def near_body(
    tile, place_ref, length_hbm, x_hbm, z_hbm, solves_hbm, signs_hbm,
    kern_ref, z_ref, stack_ref, length_ref, x_ref, solves_ref, signs_ref, sems,
):
    columns = kern_ref.shape[1]
    first = place_ref[0] * columns
    whole = pl.ds(pl.multiple_of(first, columns), columns)
    starts = range(0, columns, tile)
    copies = [
        pltpu.make_async_copy(length_hbm, length_ref, sems.at[0]),
        pltpu.make_async_copy(x_hbm, x_ref, sems.at[1]),
    ]
    for index, start in enumerate(starts):
        source = pl.ds(pl.multiple_of(first + start, tile), tile)
        copies.append(pltpu.make_async_copy(z_hbm.at[:, source], z_ref.at[:, pl.ds(start, tile)], sems.at[4 + index]))
    copies.append(pltpu.make_async_copy(solves_hbm.at[:, whole], solves_ref, sems.at[2]))
    copies.append(pltpu.make_async_copy(signs_hbm.at[:, whole], signs_ref, sems.at[3]))
    for copy in copies:
        copy.start()
    copies[0].wait()
    copies[1].wait()
    inverse = column(1.0 / length_ref[...])
    kern_tiles(tile, inverse, x_ref[...], z_ref, kern_ref, lambda index: copies[2 + index].wait())
    copies[-2].wait()
    copies[-1].wait()
    for start in starts:
        target = slice(start, start + tile)
        stack_ref[:, target] = stacked(solves_ref[:, target], signs_ref[:, target])


def far_body(tile, length_ref, x_ref, z_ref, kern_ref):
    kern_tiles(tile, column(1.0 / length_ref[...]), x_ref[...], z_ref, kern_ref, lambda index: None)


def kern_cost(rows, columns):
    return pl.CostEstimate(
        flops=2 * rows * columns * K_ROWS, bytes_accessed=2 * rows * columns, transcendentals=rows * columns
    )


def near_call(place, length, x, z, solves, signs, columns):
    rows, probes = x.shape[1], solves.shape[0]
    tile = tile_of(columns, 2048)
    operands = [pltpu.with_memory_space_constraint(value, pltpu.HBM) for value in (length, x, z, solves, signs)]
    return pl.pallas_call(
        functools.partial(near_body, tile),
        out_shape=(
            pltpu.VMEM((rows, columns), BF16),
            pltpu.VMEM((z.shape[0], columns), z.dtype),
            pltpu.VMEM((2 * probes, columns), BF16),
        ),
        in_specs=[SMEM] + [HBM] * 5,
        out_specs=(VMEM,) * 3,
        scratch_shapes=[
            pltpu.VMEM(length.shape, length.dtype),
            pltpu.VMEM(x.shape, x.dtype),
            pltpu.VMEM((probes, columns), solves.dtype),
            pltpu.VMEM((probes, columns), signs.dtype),
            pltpu.SemaphoreType.DMA((4 + columns // tile,)),
        ],
        compiler_params=pltpu.CompilerParams(vmem_limit_bytes=24 << 20),
        cost_estimate=kern_cost(rows, columns),
        name="kern_near",
    )(place, *operands)


def far_call(length, x, z):
    rows, columns = x.shape[1], z.shape[1]
    return pl.pallas_call(
        functools.partial(far_body, tile_of(columns, 2048)),
        out_shape=pltpu.VMEM((rows, columns), BF16),
        in_specs=[VMEM] * 3,
        out_specs=VMEM,
        compiler_params=pltpu.CompilerParams(vmem_limit_bytes=24 << 20),
        cost_estimate=kern_cost(rows, columns),
        name="kern_far",
    )(length, x, z)


def stack_body(tile, place_ref, near_ref, solves_ref, signs_ref, stack_ref):
    columns = stack_ref.shape[1]
    first = place_ref[0] * columns
    for start in range(0, columns, tile):
        source = pl.ds(pl.multiple_of(first + start, tile), tile)
        target = slice(start, start + tile)
        far = stacked(solves_ref[:, source], signs_ref[:, source])
        stack_ref[:, target] = jnp.concatenate([near_ref[:, target], far], axis=0)


def stack_call(place, near, solves2, signs2):
    rows, columns = near.shape
    return pl.pallas_call(
        functools.partial(stack_body, tile_of(columns, 2048)),
        out_shape=jax.ShapeDtypeStruct((2 * rows, columns), BF16),
        in_specs=[SMEM] + [VMEM] * 3,
        out_specs=VMEM,
        compiler_params=pltpu.CompilerParams(vmem_limit_bytes=16 << 20),
        cost_estimate=pl.CostEstimate(flops=4 * rows * columns, bytes_accessed=8 * rows * columns, transcendentals=0),
        name="stack",
    )(place, near, solves2, signs2)


def project_body(tile, kern_ref, stack_ref, own_ref, other_ref):
    total = None
    for start in range(0, kern_ref.shape[1], tile):
        target = slice(start, start + tile)
        term = lax.dot_general(
            kern_ref[:, target], stack_ref[:, target], (((1,), (1,)), ((), ())), preferred_element_type=F32
        )
        total = term if total is None else total + term
    total = jnp.transpose(total)
    half = total.shape[0] // 2
    own_ref[...] = total[:half]
    other_ref[...] = total[half:].astype(BF16)


def project_call(kern, stack):
    rows, columns = kern.shape
    half = stack.shape[0] // 2
    return pl.pallas_call(
        functools.partial(project_body, tile_of(columns, 2048)),
        out_shape=(jax.ShapeDtypeStruct((half, rows), F32), jax.ShapeDtypeStruct((half, rows), BF16)),
        in_specs=[VMEM] * 2,
        out_specs=(VMEM,) * 2,
        compiler_params=pltpu.CompilerParams(vmem_limit_bytes=24 << 20),
        cost_estimate=pl.CostEstimate(
            flops=4 * rows * columns * half, bytes_accessed=2 * rows * columns, transcendentals=0
        ),
        name="project",
    )(kern, stack)


def gradient_body(
    tile, p_size, group_ref, noise_ref, length_ref, z_ref, stacks, projections, data, kerns, grad_ref, weighted_ref
):
    group = group_ref[1]
    groups, halves = len(stacks), len(kerns)
    columns = grad_ref.shape[1]
    count = kerns[0].shape[0]
    dims = data[0].shape[0]
    inverse = column(1.0 / length_ref[...])
    factor = inverse * inverse / (noise_ref[0] * p_size)

    def in_order(values):
        if groups != 2:
            return values
        own, other = values
        return [jnp.where(group == 0, own, other), jnp.where(group == 0, other, own)]

    lefts, rows = [], []
    for half in range(halves):
        blocks = []
        for index in range(groups):
            parts = []
            for block in projections:
                value = block[half * groups + index].astype(F32)
                middle = value.shape[0] // 2
                parts += [value[middle:], value[:middle]]
            blocks.append(jnp.concatenate(parts, axis=0))
        lefts.append(jnp.transpose(jnp.concatenate(in_order(blocks), axis=0)).astype(BF16))
        x = data[half][...].astype(F32)
        rows.append(jnp.concatenate([x, jnp.ones((16, x.shape[1]), F32)], axis=0).astype(BF16))

    def weigh(index):
        target = slice(index * tile, (index + 1) * tile)
        stack = jnp.concatenate(in_order([ref[:, target].astype(F32) for ref in stacks]), axis=0).astype(BF16)
        for half in range(halves):
            coef = jnp.dot(lefts[half], stack, preferred_element_type=F32)
            weighted = (kerns[half][:, target].astype(F32) * coef).astype(BF16)
            weighted_ref[index % 2, half * count : (half + 1) * count, :] = weighted

    def reduce(index):
        target = slice(index * tile, (index + 1) * tile)
        total = None
        for half in range(halves):
            weighted = weighted_ref[index % 2, half * count : (half + 1) * count, :]
            term = jnp.dot(rows[half], weighted, preferred_element_type=F32)
            total = term if total is None else total + term
        z = z_ref[:, target].astype(F32)
        grad_ref[:, target] = ((total[:dims] - z * total[dims : dims + 1]) * factor).astype(grad_ref.dtype)

    tiles = columns // tile
    for index in range(tiles + 1):
        if index < tiles:
            weigh(index)
        if index > 0:
            reduce(index - 1)


def gradient_call(place, noise, length, z, stacks, projections, data, kerns, p_size, dtype):
    rows, columns = kerns[0].shape
    groups, halves = len(stacks), len(kerns)
    tile = tile_of(columns, 256)

    def body(place_ref, noise_ref, length_ref, z_ref, *refs):
        refs = list(refs)
        take = lambda size: [refs.pop(0) for _ in range(size)]
        stack_refs, projection_refs, data_refs, kern_refs = take(groups), take(2), take(halves), take(halves)
        gradient_body(
            tile, p_size, place_ref, noise_ref, length_ref, z_ref,
            stack_refs, projection_refs, data_refs, kern_refs, *refs,
        )

    return pl.pallas_call(
        body,
        out_shape=jax.ShapeDtypeStruct(z.shape, dtype),
        in_specs=[SMEM, SMEM] + [VMEM] * (2 + groups + 2 + 2 * halves),
        out_specs=VMEM,
        scratch_shapes=[pltpu.VMEM((2, halves * rows, tile), BF16)],
        compiler_params=pltpu.CompilerParams(vmem_limit_bytes=24 << 20),
        cost_estimate=pl.CostEstimate(
            flops=2 * halves * rows * columns * 128, bytes_accessed=2 * halves * rows * columns, transcendentals=0
        ),
        name="gradient",
    )(place, noise, length, z, *stacks, *projections, *data, *kerns)


def solution(mesh):
    dp, ind, probe = mesh.shape["dp"], mesh.shape["ind"], mesh.shape["probe"]
    groups = probe // 2
    halves = dp if dp <= 2 else 1
    core_swap = [(i, i ^ 1) for i in range(probe)]
    pairwise = ind & (ind - 1) == 0

    def cores(value):
        return lax.ppermute(value, "probe", core_swap)

    def from_group(shift):
        return [((i + 2 * shift) % probe, i) for i in range(probe)]

    def from_ind(shift):
        return [(i ^ shift if pairwise else (i + shift) % ind, i) for i in range(ind)]

    def on_device(data_x, inducing_z, lengthscale, noise_var, solves, probe_signs):
        columns = inducing_z.shape[1] // 2
        p_size = solves.shape[0] * probe
        place_index = lax.axis_index("probe")
        place = jnp.stack([place_index % 2, place_index // 2]).astype(jnp.int32)
        length = lengthscale.reshape(1, -1)

        solves2, signs2 = cores(solves), cores(probe_signs)
        data = [data_x]
        for _ in range(halves - 1):
            data.append(lax.ppermute(data_x, "dp", [(i, 1 - i) for i in range(dp)]))
        kern, z, near = near_call(place, length, data_x, inducing_z, solves, probe_signs, columns)
        kerns = [kern]
        stack = stack_call(place, near, solves2, signs2)
        stacks = [stack]
        for shift in range(1, groups):
            stacks.append(lax.ppermute(stack, "probe", from_group(shift)))
        own, other = project_call(kern, stack)
        for x in data[1:]:
            kerns.append(far_call(length, x, z))

        part = (own + cores(other).astype(F32)).astype(BF16)
        peers = []
        for shift in range(1, ind):
            peers.append(lax.ppermute(part, "ind", from_ind(shift)))
        block = sum([p.astype(F32) for p in peers], part.astype(F32)).astype(BF16)

        blocks = []
        for half in range(halves):
            for shift in range(groups):
                pairs = []
                for d in range(dp):
                    for source, target in from_group(shift):
                        pairs.append(((d ^ half) * probe + source, d * probe + target))
                blocks.append(block if half == 0 and shift == 0 else lax.ppermute(block, ("dp", "probe"), pairs))
        own_blocks = jnp.stack(blocks)
        other_blocks = cores(own_blocks)

        whole = halves == dp
        grad = gradient_call(
            place, noise_var, length, z, stacks, (own_blocks, other_blocks), data, kerns, p_size,
            BF16 if whole else F32,
        )
        if not whole:
            grad = lax.psum(grad, "dp").astype(BF16)
        far = cores(grad)
        lower = place[0] == 0
        return jnp.concatenate(
            [jnp.where(lower, grad, far).astype(F32), jnp.where(lower, far, grad).astype(F32)], axis=1
        )

    return jax.shard_map(
        on_device,
        mesh=mesh,
        in_specs=(P(None, "dp"), P(None, "ind"), P(), P(), P("probe", "ind"), P("probe", "ind")),
        out_specs=P(None, "ind"),
        check_vma=False,
    )
```

time: 43.8 us -> 39.4 us (0.90)
  local copies, waits for them, and re-layouts: 2.44 us -> 0.01 us
  Pallas kernels: 19 us -> 17.1 us
    unnamed x16 -> x4, local copies, waits for them, and re-layouts: 2.44 us -> 0.01 us
    pallas_call x3 -> x4, Pallas kernels: 16.1 us -> 14.8 us  [the longest x1 7.31 us: gradient_call(): pl.pallas_call(body, out_shape=jax.ShapeDtypeStruct(z.shape, dtype), in_s...]
    ppermute x5, waiting for transfers between devices: 4.1 us -> 4.76 us  [the longest x3 3.86 us: on_device(): peers.append(lax.ppermute(part, 'ind', from_ind(shift)))]
    ppermute x3, waiting for transfers between devices: 1.24 us -> 0.6 us  [on_device(): lax.ppermute(block, ('dp', 'probe'), pairs)]
    pallas_call x1, Pallas kernels: 2.9 us -> 2.35 us  [project_call(): pl.pallas_call(functools.partial(project_body, tile_of(columns, 2048)), o...]
  transfers between devices with their start and end apart: 13 -> 13, of which waited for: 6 -> 6; matrix products, arithmetic and copies ran while one was open for 0% -> 0% of each run, Pallas kernels for 16% -> 18%
where the time goes in v2:
time: 39.4 us; the launch traced here: 39.2 us
  Pallas kernels  17.1 us (43%)
  starting transfers between devices  13.3 us (34%)
  waiting for transfers between devices  6.89 us (17%)
  other arithmetic  1.18 us (3%)
  between operations  0.76 us (2%)
    pallas_call x1, Pallas kernels, gradient_call(): pl.pallas_call(body, out_shape=jax.ShapeDtypeStruct(z.shape, dtype), in_s...  7.31 us
    ppermute x3, starting transfers between devices, on_device(): peers.append(lax.ppermute(part, 'ind', from_ind(shift)))  4.45 us
    pallas_call x1, Pallas kernels, near_call(): pl.pallas_call(functools.partial(near_body, tile), out_shape=(pltpu.VMEM(...  4.4 us
    ppermute x3, waiting for transfers between devices, on_device(): peers.append(lax.ppermute(part, 'ind', from_ind(shift)))  3.86 us
    ppermute x3, starting transfers between devices, on_device(): lax.ppermute(block, ('dp', 'probe'), pairs)  3.55 us
    ppermute x1, starting transfers between devices, on_device(): stacks.append(lax.ppermute(stack, 'probe', from_group(shift)))  2.57 us
    pallas_call x1, Pallas kernels, far_call(): pl.pallas_call(functools.partial(far_body, tile_of(columns, 2048)), out_s...  2.49 us
    pallas_call x1, Pallas kernels, project_call(): pl.pallas_call(functools.partial(project_body, tile_of(columns, 2048)), o...  2.35 us
  transfers between devices with their start and end apart: 13, of which 6 were waited for; matrix products, arithmetic and copies ran while one was open for 0% of the time, Pallas kernels for 18%

profile of v2, /device:TPU:0, one launch (start us, length us, event | category | flops | bytes accessed | tf_op | source)
XLA Modules:
  0.0 39.2 jit_solution(17214286714471101436)
XLA Ops:
  0.0 0.5 %collective-permute-start.1 = (s32[8,16384]{1,0:T(8,128)}, s32[8,16384]{1,0:T(8,128)S(1)}, u32[]{:S(2)}, u32[]{:S(2)}) collective-permute-start(s32[8,16384]{1,0:T(8,128)} %signs_hbm.1), channel_id=1, source_target_pairs={{0,1},{1,0},{2,3},{3,2},{4,5},{5,4},{6,7},{7,6},{8,9},{9,8},{10,11... | collective-permute-start | bytes 1572872 | tf_op jit(solution)/shard_map/ppermute | solution.py:298
  0.5 0.0 collective-permute-start
  0.5 0.1 pad_add_fusion.place_ref
  0.6 0.0 copy-start
  0.6 0.0 copy-start.1
  0.6 4.4 %kern_near.1 = (bf16[512,8192]{1,0:T(8,128)(2,1)S(1)}, bf16[16,8192]{1,0:T(8,128)(2,1)S(1)}, bf16[16,8192]{1,0:T(8,128)(2,1)S(1)}) custom-call(s32[2]{0:T(128)S(1)} %pad_add_fusion.place_ref, f32[1,16]{1,0:T(1,128)} %bitcast.7, bf16[16,512]{1,0:T(8,128)(2,1)} %refs_4_.1, bf16[16,16384]{1,0:T(8,128)(2,1)} %z_hbm.1, bf16[8,16384]{1,0:T(8,128)(2,1)} %solves_hbm.1, ...), custom_call_target="tpu_custom_call" | custom-call | flops 1073741824 | bytes 8388608 | tf_op jit(solution)/shard_map/kern_near/pallas_call | solution.py:117
  5.0 0.0 collective-permute-done.solves_ref
  5.0 0.0 collective-permute-done.1.signs_ref
  5.0 0.6 %stack.33.stack_ref.refs_0_ = bf16[32,8192]{1,0:T(8,128)(2,1)S(1)} custom-call(s32[2]{0:T(128)S(1)} %pad_add_fusion.place_ref, bf16[16,8192]{1,0:T(8,128)(2,1)S(1)} %get-tuple-element.11.near_ref, bf16[8,16384]{1,0:T(8,128)(2,1)S(1)} %collective-permute-done.solves_ref, s32[8,16384]{1,0:T(8,128)S(1)} %collective-permute-done.1.signs_ref), custom_call_target="tpu_custom_call" | custom-call | flops 524288 | bytes 1048576 | tf_op jit(solution)/shard_map/stack/pallas_call | solution.py:164
  5.6 2.3 %project.1 = (f32[16,512]{1,0:T(8,128)S(1)}, bf16[16,512]{1,0:T(8,128)(2,1)S(1)}) custom-call(bf16[512,8192]{1,0:T(8,128)(2,1)S(1)} %get-tuple-element.12.kern_ref.refs_6_, bf16[32,8192]{1,0:T(8,128)(2,1)S(1)} %stack.33.stack_ref.refs_0_), custom_call_target="tpu_custom_call" | custom-call | flops 268435456 | bytes 8388608 | tf_op jit(solution)/shard_map/project/pallas_call | solution.py:192
  8.0 0.5 %collective-permute-start.3 = (bf16[16,512]{1,0:T(8,128)(2,1)S(1)}, bf16[16,512]{1,0:T(8,128)(2,1)S(1)}, u32[]{:S(2)}, u32[]{:S(2)}) collective-permute-start(bf16[16,512]{1,0:T(8,128)(2,1)S(1)} %get-tuple-element.14), channel_id=1, source_target_pairs={{0,1},{1,0},{2,3},{3,2},{4,5},{5,4},{6,7},{7,6},{8,9},{9,8},{10,11... | collective-permute-start | bytes 49160 | tf_op jit(solution)/shard_map/ppermute | solution.py:298
  8.5 2.6 %collective-permute-start.2 = (bf16[32,8192]{1,0:T(8,128)(2,1)S(1)}, bf16[32,8192]{1,0:T(8,128)(2,1)S(1)}, u32[]{:S(2)}, u32[]{:S(2)}) collective-permute-start(bf16[32,8192]{1,0:T(8,128)(2,1)S(1)} %stack.33.stack_ref.refs_0_), channel_id=1, source_target_pairs={{2,0},{3,1},{0,2},{1,3},{6,4},{7,5},{4,6},{5,7},{10,8},{11,9},{8,1... | collective-permute-start | bytes 1572872 | tf_op jit(solution)/shard_map/ppermute | solution.py:322
  11.1 0.0 collective-permute-done.3
  11.1 3.7 %collective-permute-start.6 = (bf16[16,512]{1,0:T(8,128)(2,1)S(1)}, bf16[16,512]{1,0:T(8,128)(2,1)S(1)}, u32[]{:S(2)}, u32[]{:S(2)}) collective-permute-start(bf16[16,512]{1,0:T(8,128)(2,1)S(1)} %add_convert_fusion.1), channel_id=1, source_target_pairs={{12,0},{8,4},{4,8},{0,12},{13,1},{9,5},{5,9},{1,13},{14,2},{10,6},... | collective-permute-start | bytes 49160 | tf_op jit(solution)/shard_map/ppermute | solution.py:330
  14.8 0.0 collective-permute-start.5
  14.8 0.8 %collective-permute-start.4 = (bf16[16,512]{1,0:T(8,128)(2,1)S(1)}, bf16[16,512]{1,0:T(8,128)(2,1)S(1)}, u32[]{:S(2)}, u32[]{:S(2)}) collective-permute-start(bf16[16,512]{1,0:T(8,128)(2,1)S(1)} %add_convert_fusion.1), channel_id=1, source_target_pairs={{4,0},{0,4},{12,8},{8,12},{5,1},{1,5},{13,9},{9,13},{6,2},{2,6},{1... | collective-permute-start | bytes 49160 | tf_op jit(solution)/shard_map/ppermute | solution.py:330
  15.5 1.1 %collective-permute-done.6 = bf16[16,512]{1,0:T(8,128)(2,1)S(1)} collective-permute-done((bf16[16,512]{1,0:T(8,128)(2,1)S(1)}, bf16[16,512]{1,0:T(8,128)(2,1)S(1)}, u32[]{:S(2)}, u32[]{:S(2)}) %collective-permute-start.6) | collective-permute-done | bytes 16416 | tf_op jit(solution)/shard_map/ppermute | solution.py:330
  16.7 2.7 %collective-permute-done.5 = bf16[16,512]{1,0:T(8,128)(2,1)S(1)} collective-permute-done((bf16[16,512]{1,0:T(8,128)(2,1)S(1)}, bf16[16,512]{1,0:T(8,128)(2,1)S(1)}, u32[]{:S(2)}, u32[]{:S(2)}) %collective-permute-start.5) | collective-permute-done | bytes 16416 | tf_op jit(solution)/shard_map/ppermute | solution.py:330
  19.4 0.0 collective-permute-done.4
  19.4 2.0 %collective-permute-start.9 = (bf16[16,512]{1,0:T(8,128)(2,1)S(1)}, bf16[16,512]{1,0:T(8,128)(2,1)S(1)}, u32[]{:S(2)}, u32[]{:S(2)}) collective-permute-start(bf16[16,512]{1,0:T(8,128)(2,1)S(1)} %add_convert_fusion), channel_id=1, source_target_pairs={{18,0},{19,1},{16,2},{17,3},{2,16},{3,17},{0,18},{1,19},{22,4},{23... | collective-permute-start | bytes 49160 | tf_op jit(solution)/shard_map/ppermute | solution.py:340
  21.4 0.5 %collective-permute-start.8 = (bf16[16,512]{1,0:T(8,128)(2,1)S(1)}, bf16[16,512]{1,0:T(8,128)(2,1)S(1)}, u32[]{:S(2)}, u32[]{:S(2)}) collective-permute-start(bf16[16,512]{1,0:T(8,128)(2,1)S(1)} %add_convert_fusion), channel_id=1, source_target_pairs={{16,0},{17,1},{18,2},{19,3},{0,16},{1,17},{2,18},{3,19},{20,4},{21... | collective-permute-start | bytes 49160 | tf_op jit(solution)/shard_map/ppermute | solution.py:340
  22.0 1.0 %collective-permute-start.7 = (bf16[16,512]{1,0:T(8,128)(2,1)S(1)}, bf16[16,512]{1,0:T(8,128)(2,1)S(1)}, u32[]{:S(2)}, u32[]{:S(2)}) collective-permute-start(bf16[16,512]{1,0:T(8,128)(2,1)S(1)} %add_convert_fusion), channel_id=1, source_target_pairs={{2,0},{3,1},{0,2},{1,3},{18,16},{19,17},{16,18},{17,19},{6,4},{7,5... | collective-permute-start | bytes 49160 | tf_op jit(solution)/shard_map/ppermute | solution.py:340
  23.0 0.0 copy-done
  23.0 1.5 %collective-permute-start.11 = (bf16[16,512]{1,0:T(8,128)(2,1)S(1)}, bf16[16,512]{1,0:T(8,128)(2,1)S(1)}, u32[]{:S(2)}, u32[]{:S(2)}) collective-permute-start(bf16[16,512]{1,0:T(8,128)(2,1)S(1)} %copy-done), channel_id=1, source_target_pairs={{0,16},{16,0},{1,17},{17,1},{2,18},{18,2},{3,19},{19,3},{4,20},{20... | collective-permute-start | bytes 49160 | tf_op jit(solution)/shard_map/ppermute | solution.py:316
  25.1 0.0 collective-permute-done.9
  25.1 0.1 collective-permute-done.8
  25.2 0.5 %collective-permute-done.7 = bf16[16,512]{1,0:T(8,128)(2,1)S(1)} collective-permute-done((bf16[16,512]{1,0:T(8,128)(2,1)S(1)}, bf16[16,512]{1,0:T(8,128)(2,1)S(1)}, u32[]{:S(2)}, u32[]{:S(2)}) %collective-permute-start.7) | collective-permute-done | bytes 16416 | tf_op jit(solution)/shard_map/ppermute | solution.py:340
  25.7 0.1 collective-permute-start.10
  25.8 0.9 %collective-permute-done.11.x_ref.refs_5_ = bf16[16,512]{1,0:T(8,128)(2,1)S(1)} collective-permute-done((bf16[16,512]{1,0:T(8,128)(2,1)S(1)}, bf16[16,512]{1,0:T(8,128)(2,1)S(1)}, u32[]{:S(2)}, u32[]{:S(2)}) %collective-permute-start.11) | collective-permute-done | bytes 16416 | tf_op jit(solution)/shard_map/ppermute | solution.py:316
  26.7 0.0 copy-done.1
  26.7 2.5 %kern_far.1.refs_7_ = bf16[512,8192]{1,0:T(8,128)(2,1)S(1)} custom-call(f32[1,16]{1,0:T(1,128)S(1)} %bitcast.8, bf16[16,512]{1,0:T(8,128)(2,1)S(1)} %collective-permute-done.11.x_ref.refs_5_, bf16[16,8192]{1,0:T(8,128)(2,1)S(1)} %get-tuple-element.10.z_ref), custom_call_target="tpu_custom_call" | custom-call | flops 1073741824 | bytes 8388608 | tf_op jit(solution)/shard_map/kern_far/pallas_call | solution.py:141
  29.2 0.0 collective-permute-done.10.refs_3_
  29.2 0.0 collective-permute-done.2.refs_1_
  29.2 7.3 %gradient.1 = bf16[16,8192]{1,0:T(8,128)(2,1)S(1)} custom-call(s32[2]{0:T(128)S(1)} %pad_add_fusion.place_ref, f32[1]{0:T(128)S(6)} %copy.7.noise_ref, f32[1,16]{1,0:T(1,128)S(1)} %bitcast.9, bf16[16,8192]{1,0:T(8,128)(2,1)S(1)} %get-tuple-element.10.z_ref, bf16[32,8192]{1,0:T(8,128)(2,1)S(1)} %stack.33.stack_ref.refs_0_, ...), custom_call_target="tpu_custom_call" | custom-call | flops 2147483648 | bytes 16777216 | tf_op jit(solution)/shard_map/gradient/pallas_call | solution.py:276
  36.5 0.1 collective-permute-start.12
  36.6 1.5 %collective-permute-done.12 = bf16[16,8192]{1,0:T(8,128)(2,1)S(1)} collective-permute-done((bf16[16,8192]{1,0:T(8,128)(2,1)S(1)}, bf16[16,8192]{1,0:T(8,128)(2,1)S(1)}, u32[]{:S(2)}, u32[]{:S(2)}) %collective-permute-start.12) | collective-permute-done | bytes 262176 | tf_op jit(solution)/shard_map/ppermute | solution.py:298
  38.2 1.0 %maximum_convert_fusion = f32[16,16384]{1,0:T(8,128)} fusion(bf16[16,8192]{1,0:T(8,128)(2,1)S(1)} %get-tuple-element.16, bf16[16,8192]{1,0:T(8,128)(2,1)S(1)} %get-tuple-element.15), kind=kLoop, calls=%fused_computation | loop fusion | flops 1048576 | bytes 1572864 | tf_op jit(solution)/shard_map/concatenate | solution.py:353
  (4 shorter events, 0.1 us)
Async XLA Ops:
  0.0 5.0 %collective-permute-start.1 = (s32[8,16384]{1,0:T(8,128)}, s32[8,16384]{1,0:T(8,128)S(1)}, u32[]{:S(2)}, u32[]{:S(2)}) collective-permute-start(s32[8,16384]{1,0:T(8,128)} %signs_hbm.1), channel_id=1, source_target_pairs={{0,1},{1,0},{2,3},{3,2},{4,5},{5,4},{6,7},{7,6},{8,9},{9,8},{10,11... | collective-permute-start | bytes 1572872 | tf_op jit(solution)/shard_map/ppermute | solution.py:298
  0.5 4.5 %collective-permute-start = (bf16[8,16384]{1,0:T(8,128)(2,1)}, bf16[8,16384]{1,0:T(8,128)(2,1)S(1)}, u32[]{:S(2)}, u32[]{:S(2)}) collective-permute-start(bf16[8,16384]{1,0:T(8,128)(2,1)} %solves_hbm.1), channel_id=1, source_target_pairs={{0,1},{1,0},{2,3},{3,2},{4,5},{5,4},{6,7},{7,6},{8,9},{9,8},{10,11... | collective-permute-start | bytes 786440 | tf_op jit(solution)/shard_map/ppermute | solution.py:298
  0.6 22.4 %copy-start = (bf16[16,512]{1,0:T(8,128)(2,1)S(1)}, bf16[16,512]{1,0:T(8,128)(2,1)}, u32[]{:S(2)}) copy-start(bf16[16,512]{1,0:T(8,128)(2,1)} %refs_4_.1) | copy-start | bytes 49156
  0.6 26.1 %copy-start.1 = (f32[16]{0:T(128)S(1)}, f32[16]{0:T(128)}, u32[]{:S(2)}) copy-start(f32[16]{0:T(128)} %param.8) | copy-start | bytes 196
  8.0 3.1 %collective-permute-start.3 = (bf16[16,512]{1,0:T(8,128)(2,1)S(1)}, bf16[16,512]{1,0:T(8,128)(2,1)S(1)}, u32[]{:S(2)}, u32[]{:S(2)}) collective-permute-start(bf16[16,512]{1,0:T(8,128)(2,1)S(1)} %get-tuple-element.14), channel_id=1, source_target_pairs={{0,1},{1,0},{2,3},{3,2},{4,5},{5,4},{6,7},{7,6},{8,9},{9,8},{10,11... | collective-permute-start | bytes 49160 | tf_op jit(solution)/shard_map/ppermute | solution.py:298
  8.5 20.7 %collective-permute-start.2 = (bf16[32,8192]{1,0:T(8,128)(2,1)S(1)}, bf16[32,8192]{1,0:T(8,128)(2,1)S(1)}, u32[]{:S(2)}, u32[]{:S(2)}) collective-permute-start(bf16[32,8192]{1,0:T(8,128)(2,1)S(1)} %stack.33.stack_ref.refs_0_), channel_id=1, source_target_pairs={{2,0},{3,1},{0,2},{1,3},{6,4},{7,5},{4,6},{5,7},{10,8},{11,9},{8,1... | collective-permute-start | bytes 1572872 | tf_op jit(solution)/shard_map/ppermute | solution.py:322
  11.1 5.6 %collective-permute-start.6 = (bf16[16,512]{1,0:T(8,128)(2,1)S(1)}, bf16[16,512]{1,0:T(8,128)(2,1)S(1)}, u32[]{:S(2)}, u32[]{:S(2)}) collective-permute-start(bf16[16,512]{1,0:T(8,128)(2,1)S(1)} %add_convert_fusion.1), channel_id=1, source_target_pairs={{12,0},{8,4},{4,8},{0,12},{13,1},{9,5},{5,9},{1,13},{14,2},{10,6},... | collective-permute-start | bytes 49160 | tf_op jit(solution)/shard_map/ppermute | solution.py:330
  14.8 4.6 %collective-permute-start.5 = (bf16[16,512]{1,0:T(8,128)(2,1)S(1)}, bf16[16,512]{1,0:T(8,128)(2,1)S(1)}, u32[]{:S(2)}, u32[]{:S(2)}) collective-permute-start(bf16[16,512]{1,0:T(8,128)(2,1)S(1)} %add_convert_fusion.1), channel_id=1, source_target_pairs={{8,0},{12,4},{0,8},{4,12},{9,1},{13,5},{1,9},{5,13},{10,2},{14,6},... | collective-permute-start | bytes 49160 | tf_op jit(solution)/shard_map/ppermute | solution.py:330
  14.8 4.6 %collective-permute-start.4 = (bf16[16,512]{1,0:T(8,128)(2,1)S(1)}, bf16[16,512]{1,0:T(8,128)(2,1)S(1)}, u32[]{:S(2)}, u32[]{:S(2)}) collective-permute-start(bf16[16,512]{1,0:T(8,128)(2,1)S(1)} %add_convert_fusion.1), channel_id=1, source_target_pairs={{4,0},{0,4},{12,8},{8,12},{5,1},{1,5},{13,9},{9,13},{6,2},{2,6},{1... | collective-permute-start | bytes 49160 | tf_op jit(solution)/shard_map/ppermute | solution.py:330
  19.4 5.7 %collective-permute-start.9 = (bf16[16,512]{1,0:T(8,128)(2,1)S(1)}, bf16[16,512]{1,0:T(8,128)(2,1)S(1)}, u32[]{:S(2)}, u32[]{:S(2)}) collective-permute-start(bf16[16,512]{1,0:T(8,128)(2,1)S(1)} %add_convert_fusion), channel_id=1, source_target_pairs={{18,0},{19,1},{16,2},{17,3},{2,16},{3,17},{0,18},{1,19},{22,4},{23... | collective-permute-start | bytes 49160 | tf_op jit(solution)/shard_map/ppermute | solution.py:340
  21.4 3.7 %collective-permute-start.8 = (bf16[16,512]{1,0:T(8,128)(2,1)S(1)}, bf16[16,512]{1,0:T(8,128)(2,1)S(1)}, u32[]{:S(2)}, u32[]{:S(2)}) collective-permute-start(bf16[16,512]{1,0:T(8,128)(2,1)S(1)} %add_convert_fusion), channel_id=1, source_target_pairs={{16,0},{17,1},{18,2},{19,3},{0,16},{1,17},{2,18},{3,19},{20,4},{21... | collective-permute-start | bytes 49160 | tf_op jit(solution)/shard_map/ppermute | solution.py:340
  22.0 3.7 %collective-permute-start.7 = (bf16[16,512]{1,0:T(8,128)(2,1)S(1)}, bf16[16,512]{1,0:T(8,128)(2,1)S(1)}, u32[]{:S(2)}, u32[]{:S(2)}) collective-permute-start(bf16[16,512]{1,0:T(8,128)(2,1)S(1)} %add_convert_fusion), channel_id=1, source_target_pairs={{2,0},{3,1},{0,2},{1,3},{18,16},{19,17},{16,18},{17,19},{6,4},{7,5... | collective-permute-start | bytes 49160 | tf_op jit(solution)/shard_map/ppermute | solution.py:340
  23.0 3.7 %collective-permute-start.11 = (bf16[16,512]{1,0:T(8,128)(2,1)S(1)}, bf16[16,512]{1,0:T(8,128)(2,1)S(1)}, u32[]{:S(2)}, u32[]{:S(2)}) collective-permute-start(bf16[16,512]{1,0:T(8,128)(2,1)S(1)} %copy-done), channel_id=1, source_target_pairs={{0,16},{16,0},{1,17},{17,1},{2,18},{18,2},{3,19},{19,3},{4,20},{20... | collective-permute-start | bytes 49160 | tf_op jit(solution)/shard_map/ppermute | solution.py:316
  25.7 3.5 %collective-permute-start.10 = (bf16[4,16,512]{2,1,0:T(8,128)(2,1)S(1)}, bf16[4,16,512]{2,1,0:T(8,128)(2,1)S(1)}, u32[]{:S(2)}, u32[]{:S(2)}) collective-permute-start(bf16[4,16,512]{2,1,0:T(8,128)(2,1)S(1)} %pad_maximum_fusion.refs_2_), channel_id=1, source_target_pairs={{0,1},{1,0},{2,3},{3,2},{4,5},{5,4},{6,7},{7,6},{8,9},{9,8},{10,11... | collective-permute-start | bytes 196616 | tf_op jit(solution)/shard_map/ppermute | solution.py:298
  36.5 1.6 %collective-permute-start.12 = (bf16[16,8192]{1,0:T(8,128)(2,1)S(1)}, bf16[16,8192]{1,0:T(8,128)(2,1)S(1)}, u32[]{:S(2)}, u32[]{:S(2)}) collective-permute-start(bf16[16,8192]{1,0:T(8,128)(2,1)S(1)} %gradient.1), channel_id=1, source_target_pairs={{0,1},{1,0},{2,3},{3,2},{4,5},{5,4},{6,7},{7,6},{8,9},{9,8},{10,11... | collective-permute-start | bytes 786440 | tf_op jit(solution)/shard_map/ppermute | solution.py:298

commit v3 on v2

--- a/solution.py
+++ b/solution.py
@@ -13,7 +13,6 @@
 BF16 = jnp.bfloat16
 VMEM = pl.BlockSpec(memory_space=pltpu.VMEM)
 HBM = pl.BlockSpec(memory_space=pltpu.HBM)
-SMEM = pl.BlockSpec(memory_space=pltpu.SMEM)
 K_ROWS = 128
 
 
@@ -61,47 +60,48 @@
     return jnp.concatenate([solves.astype(F32), (2 * signs - 1).astype(F32)], axis=0).astype(BF16)
 
 
-def kern_tiles(tile, inverse, x, z_ref, kern_ref, arrived):
+def kern_tiles(tile, inverse, x, z_ref, kern_ref, arrived=lambda index: None, beside=lambda target: None):
     left = x_side(x, inverse)
     for index in range(kern_ref.shape[1] // tile):
         arrived(index)
         target = slice(index * tile, (index + 1) * tile)
         right = z_side(z_ref[:, target], inverse)
         kern_ref[:, target] = jnp.exp2(jnp.dot(left, right, preferred_element_type=F32)).astype(BF16)
+        beside(target)
 
 
 def near_body(
-    tile, place_ref, length_hbm, x_hbm, z_hbm, solves_hbm, signs_hbm,
+    tile, length_hbm, x_hbm, z_hbm, solves_hbm, signs_hbm,
     kern_ref, z_ref, stack_ref, length_ref, x_ref, solves_ref, signs_ref, sems,
 ):
     columns = kern_ref.shape[1]
-    first = place_ref[0] * columns
+    first = (lax.axis_index("probe") % 2) * columns
     whole = pl.ds(pl.multiple_of(first, columns), columns)
-    starts = range(0, columns, tile)
     copies = [
         pltpu.make_async_copy(length_hbm, length_ref, sems.at[0]),
         pltpu.make_async_copy(x_hbm, x_ref, sems.at[1]),
     ]
-    for index, start in enumerate(starts):
-        source = pl.ds(pl.multiple_of(first + start, tile), tile)
-        copies.append(pltpu.make_async_copy(z_hbm.at[:, source], z_ref.at[:, pl.ds(start, tile)], sems.at[4 + index]))
+    copies.append(pltpu.make_async_copy(z_hbm.at[:, whole], z_ref, sems.at[4]))
     copies.append(pltpu.make_async_copy(solves_hbm.at[:, whole], solves_ref, sems.at[2]))
     copies.append(pltpu.make_async_copy(signs_hbm.at[:, whole], signs_ref, sems.at[3]))
     for copy in copies:
         copy.start()
     copies[0].wait()
     copies[1].wait()
-    inverse = column(1.0 / length_ref[...])
-    kern_tiles(tile, inverse, x_ref[...], z_ref, kern_ref, lambda index: copies[2 + index].wait())
-    copies[-2].wait()
-    copies[-1].wait()
-    for start in starts:
-        target = slice(start, start + tile)
-        stack_ref[:, target] = stacked(solves_ref[:, target], signs_ref[:, target])
+
+    def arrived(index):
+        if index == 0:
+            for copy in copies[2:]:
+                copy.wait()
+
+    def beside(target):
+        stack_ref[: 2 * solves_ref.shape[0], target] = stacked(solves_ref[:, target], signs_ref[:, target])
+
+    kern_tiles(tile, column(1.0 / length_ref[...]), x_ref[...], z_ref, kern_ref, arrived, beside)
 
 
 def far_body(tile, length_ref, x_ref, z_ref, kern_ref):
-    kern_tiles(tile, column(1.0 / length_ref[...]), x_ref[...], z_ref, kern_ref, lambda index: None)
+    kern_tiles(tile, column(1.0 / length_ref[...]), x_ref[...], z_ref, kern_ref)
 
 
 def kern_cost(rows, columns):
@@ -110,7 +110,7 @@
     )
 
 
-def near_call(place, length, x, z, solves, signs, columns):
+def near_call(length, x, z, solves, signs, columns):
     rows, probes = x.shape[1], solves.shape[0]
     tile = tile_of(columns, 2048)
     operands = [pltpu.with_memory_space_constraint(value, pltpu.HBM) for value in (length, x, z, solves, signs)]
@@ -119,21 +119,21 @@
         out_shape=(
             pltpu.VMEM((rows, columns), BF16),
             pltpu.VMEM((z.shape[0], columns), z.dtype),
-            pltpu.VMEM((2 * probes, columns), BF16),
+            pltpu.VMEM((4 * probes, columns), BF16),
         ),
-        in_specs=[SMEM] + [HBM] * 5,
+        in_specs=[HBM] * 5,
         out_specs=(VMEM,) * 3,
         scratch_shapes=[
             pltpu.VMEM(length.shape, length.dtype),
             pltpu.VMEM(x.shape, x.dtype),
             pltpu.VMEM((probes, columns), solves.dtype),
             pltpu.VMEM((probes, columns), signs.dtype),
-            pltpu.SemaphoreType.DMA((4 + columns // tile,)),
+            pltpu.SemaphoreType.DMA((5,)),
         ],
         compiler_params=pltpu.CompilerParams(vmem_limit_bytes=24 << 20),
         cost_estimate=kern_cost(rows, columns),
         name="kern_near",
-    )(place, *operands)
+    )(*operands)
 
 
 def far_call(length, x, z):
@@ -149,27 +149,27 @@
     )(length, x, z)
 
 
-def stack_body(tile, place_ref, near_ref, solves_ref, signs_ref, stack_ref):
-    columns = stack_ref.shape[1]
-    first = place_ref[0] * columns
+def stack_body(tile, near_ref, solves_ref, signs_ref, stack_ref):
+    del near_ref
+    half, columns = stack_ref.shape[0] // 2, stack_ref.shape[1]
+    first = (lax.axis_index("probe") % 2) * columns
     for start in range(0, columns, tile):
         source = pl.ds(pl.multiple_of(first + start, tile), tile)
-        target = slice(start, start + tile)
-        far = stacked(solves_ref[:, source], signs_ref[:, source])
-        stack_ref[:, target] = jnp.concatenate([near_ref[:, target], far], axis=0)
-
-
-def stack_call(place, near, solves2, signs2):
+        stack_ref[half:, start : start + tile] = stacked(solves_ref[:, source], signs_ref[:, source])
+
+
+def stack_call(near, solves2, signs2):
     rows, columns = near.shape
     return pl.pallas_call(
         functools.partial(stack_body, tile_of(columns, 2048)),
-        out_shape=jax.ShapeDtypeStruct((2 * rows, columns), BF16),
-        in_specs=[SMEM] + [VMEM] * 3,
+        out_shape=jax.ShapeDtypeStruct((rows, columns), BF16),
+        in_specs=[VMEM] * 3,
+        input_output_aliases={0: 0},
         out_specs=VMEM,
         compiler_params=pltpu.CompilerParams(vmem_limit_bytes=16 << 20),
         cost_estimate=pl.CostEstimate(flops=4 * rows * columns, bytes_accessed=8 * rows * columns, transcendentals=0),
         name="stack",
-    )(place, near, solves2, signs2)
+    )(near, solves2, signs2)
 
 
 def project_body(tile, kern_ref, stack_ref, own_ref, other_ref):
@@ -203,15 +203,15 @@
 
 
 def gradient_body(
-    tile, p_size, group_ref, noise_ref, length_ref, z_ref, stacks, projections, data, kerns, grad_ref, weighted_ref
+    tile, p_size, noise_ref, length_ref, z_ref, stacks, projections, data, kerns, grad_ref, weighted_ref
 ):
-    group = group_ref[1]
+    group = lax.axis_index("probe") // 2
     groups, halves = len(stacks), len(kerns)
     columns = grad_ref.shape[1]
     count = kerns[0].shape[0]
     dims = data[0].shape[0]
     inverse = column(1.0 / length_ref[...])
-    factor = inverse * inverse / (noise_ref[0] * p_size)
+    factor = inverse * inverse / (noise_ref[...] * p_size)
 
     def in_order(values):
         if groups != 2:
@@ -259,24 +259,24 @@
             reduce(index - 1)
 
 
-def gradient_call(place, noise, length, z, stacks, projections, data, kerns, p_size, dtype):
+def gradient_call(noise, length, z, stacks, projections, data, kerns, p_size, dtype):
     rows, columns = kerns[0].shape
     groups, halves = len(stacks), len(kerns)
     tile = tile_of(columns, 256)
 
-    def body(place_ref, noise_ref, length_ref, z_ref, *refs):
+    def body(noise_ref, length_ref, z_ref, *refs):
         refs = list(refs)
         take = lambda size: [refs.pop(0) for _ in range(size)]
         stack_refs, projection_refs, data_refs, kern_refs = take(groups), take(2), take(halves), take(halves)
         gradient_body(
-            tile, p_size, place_ref, noise_ref, length_ref, z_ref,
+            tile, p_size, noise_ref, length_ref, z_ref,
             stack_refs, projection_refs, data_refs, kern_refs, *refs,
         )
 
     return pl.pallas_call(
         body,
         out_shape=jax.ShapeDtypeStruct(z.shape, dtype),
-        in_specs=[SMEM, SMEM] + [VMEM] * (2 + groups + 2 + 2 * halves),
+        in_specs=[VMEM] * (3 + groups + 2 + 2 * halves),
         out_specs=VMEM,
         scratch_shapes=[pltpu.VMEM((2, halves * rows, tile), BF16)],
         compiler_params=pltpu.CompilerParams(vmem_limit_bytes=24 << 20),
@@ -284,7 +284,7 @@
             flops=2 * halves * rows * columns * 128, bytes_accessed=2 * halves * rows * columns, transcendentals=0
         ),
         name="gradient",
-    )(place, noise, length, z, *stacks, *projections, *data, *kerns)
+    )(noise, length, z, *stacks, *projections, *data, *kerns)
 
 
 def solution(mesh):
@@ -306,17 +306,15 @@
     def on_device(data_x, inducing_z, lengthscale, noise_var, solves, probe_signs):
         columns = inducing_z.shape[1] // 2
         p_size = solves.shape[0] * probe
-        place_index = lax.axis_index("probe")
-        place = jnp.stack([place_index % 2, place_index // 2]).astype(jnp.int32)
         length = lengthscale.reshape(1, -1)
 
         solves2, signs2 = cores(solves), cores(probe_signs)
         data = [data_x]
         for _ in range(halves - 1):
             data.append(lax.ppermute(data_x, "dp", [(i, 1 - i) for i in range(dp)]))
-        kern, z, near = near_call(place, length, data_x, inducing_z, solves, probe_signs, columns)
+        kern, z, near = near_call(length, data_x, inducing_z, solves, probe_signs, columns)
         kerns = [kern]
-        stack = stack_call(place, near, solves2, signs2)
+        stack = stack_call(near, solves2, signs2)
         stacks = [stack]
         for shift in range(1, groups):
             stacks.append(lax.ppermute(stack, "probe", from_group(shift)))
@@ -343,13 +341,13 @@
 
         whole = halves == dp
         grad = gradient_call(
-            place, noise_var, length, z, stacks, (own_blocks, other_blocks), data, kerns, p_size,
+            noise_var.reshape(1, 1), length, z, stacks, (own_blocks, other_blocks), data, kerns, p_size,
             BF16 if whole else F32,
         )
         if not whole:
             grad = lax.psum(grad, "dp").astype(BF16)
         far = cores(grad)
-        lower = place[0] == 0
+        lower = lax.axis_index("probe") % 2 == 0
         return jnp.concatenate(
             [jnp.where(lower, grad, far).astype(F32), jnp.where(lower, far, grad).astype(F32)], axis=1
         )

time: 39.4 us -> 39.1 us (level)
  Pallas kernels: 17.1 us -> 15.3 us
  waiting for transfers between devices: 6.89 us -> 8 us
  starting transfers between devices: 13.3 us -> 13.8 us
    ppermute x3, waiting for transfers between devices: 3.86 us -> 5.31 us  [on_device(): peers.append(lax.ppermute(part, 'ind', from_ind(shift)))]
    ppermute x3, waiting for transfers between devices: 0.6 us -> 1.51 us  [on_device(): lax.ppermute(block, ('dp', 'probe'), pairs)]
    ppermute x1, waiting for transfers between devices: 0.9 us -> 0.01 us  [on_device(): data.append(lax.ppermute(data_x, 'dp', [(i, 1 - i) for i in range(dp)]))]
    pallas_call x1, Pallas kernels: 4.4 us -> 3.55 us  [near_call(): pl.pallas_call(functools.partial(near_body, tile), out_shape=(pltpu.VMEM(...]
    pallas_call x1, Pallas kernels: 0.59 us -> 0.05 us  [stack_call(): pl.pallas_call(functools.partial(stack_body, tile_of(columns, 2048)), out...]
    ppermute x5, starting transfers between devices: 1.2 us -> 1.67 us  [cores(): return lax.ppermute(value, 'probe', core_swap)]
    pallas_call x1, Pallas kernels: 7.31 us -> 6.86 us  [gradient_call(): pl.pallas_call(body, out_shape=jax.ShapeDtypeStruct(z.shape, dtype), in_s...]
  transfers between devices with their start and end apart: 13 -> 13, of which waited for: 6 -> 4; matrix products, arithmetic and copies ran while one was open for 0% -> 0% of each run, Pallas kernels for 18% -> 16%
where the time goes in v3:
time: 39.1 us; the launch traced here: 38.9 us
  Pallas kernels  15.3 us (39%)
  starting transfers between devices  13.8 us (35%)
  waiting for transfers between devices  8 us (20%)
  other arithmetic  1.11 us (3%)
  between operations  0.77 us (2%)
    pallas_call x1, Pallas kernels, gradient_call(): pl.pallas_call(body, out_shape=jax.ShapeDtypeStruct(z.shape, dtype), in_s...  6.86 us
    ppermute x3, waiting for transfers between devices, on_device(): peers.append(lax.ppermute(part, 'ind', from_ind(shift)))  5.31 us
    ppermute x3, starting transfers between devices, on_device(): peers.append(lax.ppermute(part, 'ind', from_ind(shift)))  4.45 us
    ppermute x3, starting transfers between devices, on_device(): lax.ppermute(block, ('dp', 'probe'), pairs)  3.55 us
    pallas_call x1, Pallas kernels, near_call(): pl.pallas_call(functools.partial(near_body, tile), out_shape=(pltpu.VMEM(...  3.55 us
    ppermute x1, starting transfers between devices, on_device(): stacks.append(lax.ppermute(stack, 'probe', from_group(shift)))  2.59 us
    pallas_call x1, Pallas kernels, far_call(): pl.pallas_call(functools.partial(far_body, tile_of(columns, 2048)), out_s...  2.49 us
    pallas_call x1, Pallas kernels, project_call(): pl.pallas_call(functools.partial(project_body, tile_of(columns, 2048)), o...  2.34 us
  transfers between devices with their start and end apart: 13, of which 4 were waited for; matrix products, arithmetic and copies ran while one was open for 0% of the time, Pallas kernels for 16%

profile of v3, /device:TPU:0, one launch (start us, length us, event | category | flops | bytes accessed | tf_op | source)
XLA Modules:
  0.0 38.9 jit_solution(1498838959105760701)
XLA Ops:
  0.0 0.5 %collective-permute-start.1 = (s32[8,16384]{1,0:T(8,128)}, s32[8,16384]{1,0:T(8,128)S(1)}, u32[]{:S(2)}, u32[]{:S(2)}) collective-permute-start(s32[8,16384]{1,0:T(8,128)} %signs_hbm.1), channel_id=1, source_target_pairs={{0,1},{1,0},{2,3},{3,2},{4,5},{5,4},{6,7},{7,6},{8,9},{9,8},{10,11... | collective-permute-start | bytes 1572872 | tf_op jit(solution)/shard_map/ppermute | solution.py:298
  0.5 0.0 collective-permute-start
  0.5 0.0 copy-start
  0.5 0.0 copy-start.1
  0.5 3.5 %kern_near.1 = (bf16[512,8192]{1,0:T(8,128)(2,1)S(1)}, bf16[16,8192]{1,0:T(8,128)(2,1)S(1)}, bf16[32,8192]{1,0:T(8,128)(2,1)S(1)}) custom-call(f32[1,16]{1,0:T(1,128)} %bitcast.7, bf16[16,512]{1,0:T(8,128)(2,1)} %refs_4_.1, bf16[16,16384]{1,0:T(8,128)(2,1)} %z_hbm.1, bf16[8,16384]{1,0:T(8,128)(2,1)} %solves_hbm.1, s32[8,16384]{1,0:T(8,128)} %signs_hbm.1), custom_call_target="tpu_custom_call" | custom-call | flops 1073741824 | bytes 8388608 | tf_op jit(solution)/shard_map/kern_near/pallas_call | solution.py:117
  4.1 0.0 collective-permute-done.solves_ref
  4.1 0.0 collective-permute-done.1.signs_ref
  4.1 0.1 stack.21.stack_ref.refs_0_
  4.2 2.3 %project.1 = (f32[16,512]{1,0:T(8,128)S(1)}, bf16[16,512]{1,0:T(8,128)(2,1)S(1)}) custom-call(bf16[512,8192]{1,0:T(8,128)(2,1)S(1)} %get-tuple-element.12.kern_ref.refs_6_, bf16[32,8192]{1,0:T(8,128)(2,1)S(1)} %stack.21.stack_ref.refs_0_), custom_call_target="tpu_custom_call" | custom-call | flops 268435456 | bytes 8388608 | tf_op jit(solution)/shard_map/project/pallas_call | solution.py:192
  6.5 0.5 %collective-permute-start.3 = (bf16[16,512]{1,0:T(8,128)(2,1)S(1)}, bf16[16,512]{1,0:T(8,128)(2,1)S(1)}, u32[]{:S(2)}, u32[]{:S(2)}) collective-permute-start(bf16[16,512]{1,0:T(8,128)(2,1)S(1)} %get-tuple-element.14), channel_id=1, source_target_pairs={{0,1},{1,0},{2,3},{3,2},{4,5},{5,4},{6,7},{7,6},{8,9},{9,8},{10,11... | collective-permute-start | bytes 49160 | tf_op jit(solution)/shard_map/ppermute | solution.py:298
  7.0 2.6 %collective-permute-start.2 = (bf16[32,8192]{1,0:T(8,128)(2,1)S(1)}, bf16[32,8192]{1,0:T(8,128)(2,1)S(1)}, u32[]{:S(2)}, u32[]{:S(2)}) collective-permute-start(bf16[32,8192]{1,0:T(8,128)(2,1)S(1)} %stack.21.stack_ref.refs_0_), channel_id=1, source_target_pairs={{2,0},{3,1},{0,2},{1,3},{6,4},{7,5},{4,6},{5,7},{10,8},{11,9},{8,1... | collective-permute-start | bytes 1572872 | tf_op jit(solution)/shard_map/ppermute | solution.py:320
  9.6 0.0 collective-permute-done.3
  9.6 1.6 %collective-permute-start.4 = (bf16[16,512]{1,0:T(8,128)(2,1)S(1)}, bf16[16,512]{1,0:T(8,128)(2,1)S(1)}, u32[]{:S(2)}, u32[]{:S(2)}) collective-permute-start(bf16[16,512]{1,0:T(8,128)(2,1)S(1)} %add_convert_fusion.1), channel_id=1, source_target_pairs={{4,0},{0,4},{12,8},{8,12},{5,1},{1,5},{13,9},{9,13},{6,2},{2,6},{1... | collective-permute-start | bytes 49160 | tf_op jit(solution)/shard_map/ppermute | solution.py:328
  11.3 2.6 %collective-permute-start.5 = (bf16[16,512]{1,0:T(8,128)(2,1)S(1)}, bf16[16,512]{1,0:T(8,128)(2,1)S(1)}, u32[]{:S(2)}, u32[]{:S(2)}) collective-permute-start(bf16[16,512]{1,0:T(8,128)(2,1)S(1)} %add_convert_fusion.1), channel_id=1, source_target_pairs={{8,0},{12,4},{0,8},{4,12},{9,1},{13,5},{1,9},{5,13},{10,2},{14,6},... | collective-permute-start | bytes 49160 | tf_op jit(solution)/shard_map/ppermute | solution.py:328
  13.8 0.2 collective-permute-start.6
  14.1 0.0 collective-permute-done.4
  14.1 1.9 %collective-permute-done.5 = bf16[16,512]{1,0:T(8,128)(2,1)S(1)} collective-permute-done((bf16[16,512]{1,0:T(8,128)(2,1)S(1)}, bf16[16,512]{1,0:T(8,128)(2,1)S(1)}, u32[]{:S(2)}, u32[]{:S(2)}) %collective-permute-start.5) | collective-permute-done | bytes 16416 | tf_op jit(solution)/shard_map/ppermute | solution.py:328
  16.0 3.4 %collective-permute-done.6 = bf16[16,512]{1,0:T(8,128)(2,1)S(1)} collective-permute-done((bf16[16,512]{1,0:T(8,128)(2,1)S(1)}, bf16[16,512]{1,0:T(8,128)(2,1)S(1)}, u32[]{:S(2)}, u32[]{:S(2)}) %collective-permute-start.6) | collective-permute-done | bytes 16416 | tf_op jit(solution)/shard_map/ppermute | solution.py:328
  19.4 1.1 %collective-permute-start.7 = (bf16[16,512]{1,0:T(8,128)(2,1)S(1)}, bf16[16,512]{1,0:T(8,128)(2,1)S(1)}, u32[]{:S(2)}, u32[]{:S(2)}) collective-permute-start(bf16[16,512]{1,0:T(8,128)(2,1)S(1)} %add_convert_fusion), channel_id=1, source_target_pairs={{2,0},{3,1},{0,2},{1,3},{18,16},{19,17},{16,18},{17,19},{6,4},{7,5... | collective-permute-start | bytes 49160 | tf_op jit(solution)/shard_map/ppermute | solution.py:338
  20.5 1.5 %collective-permute-start.8 = (bf16[16,512]{1,0:T(8,128)(2,1)S(1)}, bf16[16,512]{1,0:T(8,128)(2,1)S(1)}, u32[]{:S(2)}, u32[]{:S(2)}) collective-permute-start(bf16[16,512]{1,0:T(8,128)(2,1)S(1)} %add_convert_fusion), channel_id=1, source_target_pairs={{16,0},{17,1},{18,2},{19,3},{0,16},{1,17},{2,18},{3,19},{20,4},{21... | collective-permute-start | bytes 49160 | tf_op jit(solution)/shard_map/ppermute | solution.py:338
  22.0 1.0 %collective-permute-start.9 = (bf16[16,512]{1,0:T(8,128)(2,1)S(1)}, bf16[16,512]{1,0:T(8,128)(2,1)S(1)}, u32[]{:S(2)}, u32[]{:S(2)}) collective-permute-start(bf16[16,512]{1,0:T(8,128)(2,1)S(1)} %add_convert_fusion), channel_id=1, source_target_pairs={{18,0},{19,1},{16,2},{17,3},{2,16},{3,17},{0,18},{1,19},{22,4},{23... | collective-permute-start | bytes 49160 | tf_op jit(solution)/shard_map/ppermute | solution.py:338
  23.0 0.0 copy-done
  23.0 1.5 %collective-permute-start.11 = (bf16[16,512]{1,0:T(8,128)(2,1)S(1)}, bf16[16,512]{1,0:T(8,128)(2,1)S(1)}, u32[]{:S(2)}, u32[]{:S(2)}) collective-permute-start(bf16[16,512]{1,0:T(8,128)(2,1)S(1)} %copy-done), channel_id=1, source_target_pairs={{0,16},{16,0},{1,17},{17,1},{2,18},{18,2},{3,19},{19,3},{4,20},{20... | collective-permute-start | bytes 49160 | tf_op jit(solution)/shard_map/ppermute | solution.py:314
  25.1 0.0 collective-permute-done.7
  25.1 0.0 collective-permute-done.8
  25.1 1.5 %collective-permute-done.9 = bf16[16,512]{1,0:T(8,128)(2,1)S(1)} collective-permute-done((bf16[16,512]{1,0:T(8,128)(2,1)S(1)}, bf16[16,512]{1,0:T(8,128)(2,1)S(1)}, u32[]{:S(2)}, u32[]{:S(2)}) %collective-permute-start.9) | collective-permute-done | bytes 16416 | tf_op jit(solution)/shard_map/ppermute | solution.py:338
  26.7 0.1 collective-permute-start.10
  26.7 0.0 collective-permute-done.11.x_ref.refs_5_
  26.7 0.0 copy-done.1
  26.8 2.5 %kern_far.1.refs_7_ = bf16[512,8192]{1,0:T(8,128)(2,1)S(1)} custom-call(f32[1,16]{1,0:T(1,128)S(1)} %bitcast.8, bf16[16,512]{1,0:T(8,128)(2,1)S(1)} %collective-permute-done.11.x_ref.refs_5_, bf16[16,8192]{1,0:T(8,128)(2,1)S(1)} %get-tuple-element.10.z_ref), custom_call_target="tpu_custom_call" | custom-call | flops 1073741824 | bytes 8388608 | tf_op jit(solution)/shard_map/kern_far/pallas_call | solution.py:141
  29.2 0.0 collective-permute-done.10.refs_3_
  29.3 0.0 collective-permute-done.2.refs_1_
  29.3 6.9 %gradient.1 = bf16[16,8192]{1,0:T(8,128)(2,1)S(1)} custom-call(f32[1,1]{1,0:T(1,128)} %bitcast.6.noise_ref, f32[1,16]{1,0:T(1,128)S(1)} %bitcast.9, bf16[16,8192]{1,0:T(8,128)(2,1)S(1)} %get-tuple-element.10.z_ref, bf16[32,8192]{1,0:T(8,128)(2,1)S(1)} %stack.21.stack_ref.refs_0_, bf16[32,8192]{1,0:T(8,128)(2,1)S(1)} %collective-permute-done.2.refs_1_, ...), custom_call_target="tpu_custom_call" | custom-call | flops 2147483648 | bytes 16777216 | tf_op jit(solution)/shard_map/gradient/pallas_call | solution.py:276
  36.1 0.6 %collective-permute-start.12 = (bf16[16,8192]{1,0:T(8,128)(2,1)S(1)}, bf16[16,8192]{1,0:T(8,128)(2,1)S(1)}, u32[]{:S(2)}, u32[]{:S(2)}) collective-permute-start(bf16[16,8192]{1,0:T(8,128)(2,1)S(1)} %gradient.1), channel_id=1, source_target_pairs={{0,1},{1,0},{2,3},{3,2},{4,5},{5,4},{6,7},{7,6},{8,9},{9,8},{10,11... | collective-permute-start | bytes 786440 | tf_op jit(solution)/shard_map/ppermute | solution.py:298
  36.7 1.2 %collective-permute-done.12 = bf16[16,8192]{1,0:T(8,128)(2,1)S(1)} collective-permute-done((bf16[16,8192]{1,0:T(8,128)(2,1)S(1)}, bf16[16,8192]{1,0:T(8,128)(2,1)S(1)}, u32[]{:S(2)}, u32[]{:S(2)}) %collective-permute-start.12) | collective-permute-done | bytes 262176 | tf_op jit(solution)/shard_map/ppermute | solution.py:298
  37.9 1.0 %maximum_convert_fusion = f32[16,16384]{1,0:T(8,128)} fusion(bf16[16,8192]{1,0:T(8,128)(2,1)S(1)} %get-tuple-element.16, bf16[16,8192]{1,0:T(8,128)(2,1)S(1)} %get-tuple-element.15), kind=kLoop, calls=%fused_computation | loop fusion | flops 1048576 | bytes 1572864 | tf_op jit(solution)/shard_map/concatenate | solution.py:351
  (4 shorter events, 0.1 us)
Async XLA Ops:
  0.0 4.1 %collective-permute-start.1 = (s32[8,16384]{1,0:T(8,128)}, s32[8,16384]{1,0:T(8,128)S(1)}, u32[]{:S(2)}, u32[]{:S(2)}) collective-permute-start(s32[8,16384]{1,0:T(8,128)} %signs_hbm.1), channel_id=1, source_target_pairs={{0,1},{1,0},{2,3},{3,2},{4,5},{5,4},{6,7},{7,6},{8,9},{9,8},{10,11... | collective-permute-start | bytes 1572872 | tf_op jit(solution)/shard_map/ppermute | solution.py:298
  0.5 3.6 %collective-permute-start = (bf16[8,16384]{1,0:T(8,128)(2,1)}, bf16[8,16384]{1,0:T(8,128)(2,1)S(1)}, u32[]{:S(2)}, u32[]{:S(2)}) collective-permute-start(bf16[8,16384]{1,0:T(8,128)(2,1)} %solves_hbm.1), channel_id=1, source_target_pairs={{0,1},{1,0},{2,3},{3,2},{4,5},{5,4},{6,7},{7,6},{8,9},{9,8},{10,11... | collective-permute-start | bytes 786440 | tf_op jit(solution)/shard_map/ppermute | solution.py:298
  0.5 22.4 %copy-start = (bf16[16,512]{1,0:T(8,128)(2,1)S(1)}, bf16[16,512]{1,0:T(8,128)(2,1)}, u32[]{:S(2)}) copy-start(bf16[16,512]{1,0:T(8,128)(2,1)} %refs_4_.1) | copy-start | bytes 49156
  0.5 26.2 %copy-start.1 = (f32[16]{0:T(128)S(1)}, f32[16]{0:T(128)}, u32[]{:S(2)}) copy-start(f32[16]{0:T(128)} %param.8) | copy-start | bytes 196
  6.5 3.1 %collective-permute-start.3 = (bf16[16,512]{1,0:T(8,128)(2,1)S(1)}, bf16[16,512]{1,0:T(8,128)(2,1)S(1)}, u32[]{:S(2)}, u32[]{:S(2)}) collective-permute-start(bf16[16,512]{1,0:T(8,128)(2,1)S(1)} %get-tuple-element.14), channel_id=1, source_target_pairs={{0,1},{1,0},{2,3},{3,2},{4,5},{5,4},{6,7},{7,6},{8,9},{9,8},{10,11... | collective-permute-start | bytes 49160 | tf_op jit(solution)/shard_map/ppermute | solution.py:298
  7.0 22.2 %collective-permute-start.2 = (bf16[32,8192]{1,0:T(8,128)(2,1)S(1)}, bf16[32,8192]{1,0:T(8,128)(2,1)S(1)}, u32[]{:S(2)}, u32[]{:S(2)}) collective-permute-start(bf16[32,8192]{1,0:T(8,128)(2,1)S(1)} %stack.21.stack_ref.refs_0_), channel_id=1, source_target_pairs={{2,0},{3,1},{0,2},{1,3},{6,4},{7,5},{4,6},{5,7},{10,8},{11,9},{8,1... | collective-permute-start | bytes 1572872 | tf_op jit(solution)/shard_map/ppermute | solution.py:320
  9.6 4.5 %collective-permute-start.4 = (bf16[16,512]{1,0:T(8,128)(2,1)S(1)}, bf16[16,512]{1,0:T(8,128)(2,1)S(1)}, u32[]{:S(2)}, u32[]{:S(2)}) collective-permute-start(bf16[16,512]{1,0:T(8,128)(2,1)S(1)} %add_convert_fusion.1), channel_id=1, source_target_pairs={{4,0},{0,4},{12,8},{8,12},{5,1},{1,5},{13,9},{9,13},{6,2},{2,6},{1... | collective-permute-start | bytes 49160 | tf_op jit(solution)/shard_map/ppermute | solution.py:328
  11.3 4.7 %collective-permute-start.5 = (bf16[16,512]{1,0:T(8,128)(2,1)S(1)}, bf16[16,512]{1,0:T(8,128)(2,1)S(1)}, u32[]{:S(2)}, u32[]{:S(2)}) collective-permute-start(bf16[16,512]{1,0:T(8,128)(2,1)S(1)} %add_convert_fusion.1), channel_id=1, source_target_pairs={{8,0},{12,4},{0,8},{4,12},{9,1},{13,5},{1,9},{5,13},{10,2},{14,6},... | collective-permute-start | bytes 49160 | tf_op jit(solution)/shard_map/ppermute | solution.py:328
  13.8 5.5 %collective-permute-start.6 = (bf16[16,512]{1,0:T(8,128)(2,1)S(1)}, bf16[16,512]{1,0:T(8,128)(2,1)S(1)}, u32[]{:S(2)}, u32[]{:S(2)}) collective-permute-start(bf16[16,512]{1,0:T(8,128)(2,1)S(1)} %add_convert_fusion.1), channel_id=1, source_target_pairs={{12,0},{8,4},{4,8},{0,12},{13,1},{9,5},{5,9},{1,13},{14,2},{10,6},... | collective-permute-start | bytes 49160 | tf_op jit(solution)/shard_map/ppermute | solution.py:328
  19.4 5.7 %collective-permute-start.7 = (bf16[16,512]{1,0:T(8,128)(2,1)S(1)}, bf16[16,512]{1,0:T(8,128)(2,1)S(1)}, u32[]{:S(2)}, u32[]{:S(2)}) collective-permute-start(bf16[16,512]{1,0:T(8,128)(2,1)S(1)} %add_convert_fusion), channel_id=1, source_target_pairs={{2,0},{3,1},{0,2},{1,3},{18,16},{19,17},{16,18},{17,19},{6,4},{7,5... | collective-permute-start | bytes 49160 | tf_op jit(solution)/shard_map/ppermute | solution.py:338
  20.5 4.6 %collective-permute-start.8 = (bf16[16,512]{1,0:T(8,128)(2,1)S(1)}, bf16[16,512]{1,0:T(8,128)(2,1)S(1)}, u32[]{:S(2)}, u32[]{:S(2)}) collective-permute-start(bf16[16,512]{1,0:T(8,128)(2,1)S(1)} %add_convert_fusion), channel_id=1, source_target_pairs={{16,0},{17,1},{18,2},{19,3},{0,16},{1,17},{2,18},{3,19},{20,4},{21... | collective-permute-start | bytes 49160 | tf_op jit(solution)/shard_map/ppermute | solution.py:338
  22.0 4.6 %collective-permute-start.9 = (bf16[16,512]{1,0:T(8,128)(2,1)S(1)}, bf16[16,512]{1,0:T(8,128)(2,1)S(1)}, u32[]{:S(2)}, u32[]{:S(2)}) collective-permute-start(bf16[16,512]{1,0:T(8,128)(2,1)S(1)} %add_convert_fusion), channel_id=1, source_target_pairs={{18,0},{19,1},{16,2},{17,3},{2,16},{3,17},{0,18},{1,19},{22,4},{23... | collective-permute-start | bytes 49160 | tf_op jit(solution)/shard_map/ppermute | solution.py:338
  23.0 3.8 %collective-permute-start.11 = (bf16[16,512]{1,0:T(8,128)(2,1)S(1)}, bf16[16,512]{1,0:T(8,128)(2,1)S(1)}, u32[]{:S(2)}, u32[]{:S(2)}) collective-permute-start(bf16[16,512]{1,0:T(8,128)(2,1)S(1)} %copy-done), channel_id=1, source_target_pairs={{0,16},{16,0},{1,17},{17,1},{2,18},{18,2},{3,19},{19,3},{4,20},{20... | collective-permute-start | bytes 49160 | tf_op jit(solution)/shard_map/ppermute | solution.py:314
  26.7 2.6 %collective-permute-start.10 = (bf16[4,16,512]{2,1,0:T(8,128)(2,1)S(1)}, bf16[4,16,512]{2,1,0:T(8,128)(2,1)S(1)}, u32[]{:S(2)}, u32[]{:S(2)}) collective-permute-start(bf16[4,16,512]{2,1,0:T(8,128)(2,1)S(1)} %pad_maximum_fusion.refs_2_), channel_id=1, source_target_pairs={{0,1},{1,0},{2,3},{3,2},{4,5},{5,4},{6,7},{7,6},{8,9},{9,8},{10,11... | collective-permute-start | bytes 196616 | tf_op jit(solution)/shard_map/ppermute | solution.py:298
  36.1 1.7 %collective-permute-start.12 = (bf16[16,8192]{1,0:T(8,128)(2,1)S(1)}, bf16[16,8192]{1,0:T(8,128)(2,1)S(1)}, u32[]{:S(2)}, u32[]{:S(2)}) collective-permute-start(bf16[16,8192]{1,0:T(8,128)(2,1)S(1)} %gradient.1), channel_id=1, source_target_pairs={{0,1},{1,0},{2,3},{3,2},{4,5},{5,4},{6,7},{7,6},{8,9},{9,8},{10,11... | collective-permute-start | bytes 786440 | tf_op jit(solution)/shard_map/ppermute | solution.py:298

commit v4 on v3

--- a/solution.py
+++ b/solution.py
@@ -287,6 +287,39 @@
     )(noise, length, z, *stacks, *projections, *data, *kerns)
 
 
+def write_body(tile, other, grad_ref, *refs):
+    out_ref, wide_ref, sems = refs[-3:]
+    columns = grad_ref.shape[1]
+    core = lax.axis_index("probe") % 2
+    first = (1 - core if other else core) * columns
+    copies = []
+    for index in range(columns // tile):
+        source = pl.ds(index * tile, tile)
+        target = pl.ds(pl.multiple_of(first + index * tile, tile), tile)
+        wide_ref[:, source] = grad_ref[:, source].astype(F32)
+        copies.append(pltpu.make_async_copy(wide_ref.at[:, source], out_ref.at[:, target], sems.at[index]))
+        copies[-1].start()
+    for copy in copies:
+        copy.wait()
+
+
+def write_call(grad, out=None):
+    rows, columns = grad.shape
+    tile = tile_of(columns, 2048)
+    other = out is not None
+    return pl.pallas_call(
+        functools.partial(write_body, tile, other),
+        out_shape=jax.ShapeDtypeStruct((rows, 2 * columns), F32),
+        in_specs=[VMEM] + [HBM] * other,
+        out_specs=HBM,
+        scratch_shapes=[pltpu.VMEM((rows, columns), F32), pltpu.SemaphoreType.DMA((columns // tile,))],
+        input_output_aliases={1: 0} if other else {},
+        compiler_params=pltpu.CompilerParams(vmem_limit_bytes=16 << 20),
+        cost_estimate=pl.CostEstimate(flops=rows * columns, bytes_accessed=6 * rows * columns, transcendentals=0),
+        name="write_other" if other else "write_own",
+    )(grad, *([out] if other else []))
+
+
 def solution(mesh):
     dp, ind, probe = mesh.shape["dp"], mesh.shape["ind"], mesh.shape["probe"]
     groups = probe // 2
@@ -347,10 +380,8 @@
         if not whole:
             grad = lax.psum(grad, "dp").astype(BF16)
         far = cores(grad)
-        lower = lax.axis_index("probe") % 2 == 0
-        return jnp.concatenate(
-            [jnp.where(lower, grad, far).astype(F32), jnp.where(lower, far, grad).astype(F32)], axis=1
-        )
+        out = write_call(grad)
+        return write_call(far, out)
 
     return jax.shard_map(
         on_device,

time: 39.1 us -> 37.2 us (0.951)
  waiting for transfers between devices: 8 us -> 6.03 us
  Pallas kernels: 15.3 us -> 16.9 us
  other arithmetic: 1.11 us -> 0.03 us
  starting transfers between devices: 13.8 us -> 13.3 us
    pallas_call x0 -> x2, Pallas kernels: none -> 1.66 us  [write_call(): pl.pallas_call(functools.partial(write_body, tile, other), out_shape=jax....]
    ppermute x3, waiting for transfers between devices: 5.31 us -> 3.85 us  [on_device(): peers.append(lax.ppermute(part, 'ind', from_ind(shift)))]
    concatenate x1 -> x0, other arithmetic: 1.04 us -> none  [on_device(): jnp.concatenate([jnp.where(lower, grad, far).astype(F32), jnp.where(lower...]
    ppermute x3, waiting for transfers between devices: 1.51 us -> 0.59 us  [on_device(): lax.ppermute(block, ('dp', 'probe'), pairs)]
    ppermute x1, waiting for transfers between devices: 0.01 us -> 0.9 us  [on_device(): data.append(lax.ppermute(data_x, 'dp', [(i, 1 - i) for i in range(dp)]))]
    ppermute x5, starting transfers between devices: 1.67 us -> 1.19 us  [cores(): return lax.ppermute(value, 'probe', core_swap)]
    ppermute x5, waiting for transfers between devices: 1.17 us -> 0.69 us  [cores(): return lax.ppermute(value, 'probe', core_swap)]
  transfers between devices with their start and end apart: 13 -> 13, of which waited for: 4 -> 6; matrix products, arithmetic and copies ran while one was open for 0% -> 0% of each run, Pallas kernels for 16% -> 19%
where the time goes in v4:
time: 37.2 us; the launch traced here: 37 us
  Pallas kernels  16.9 us (45%)
  starting transfers between devices  13.3 us (36%)
  waiting for transfers between devices  6.03 us (16%)
  between operations  0.76 us (2%)
    pallas_call x1, Pallas kernels, gradient_call(): pl.pallas_call(body, out_shape=jax.ShapeDtypeStruct(z.shape, dtype), in_s...  6.86 us
    ppermute x3, starting transfers between devices, on_device(): peers.append(lax.ppermute(part, 'ind', from_ind(shift)))  4.45 us
    ppermute x3, waiting for transfers between devices, on_device(): peers.append(lax.ppermute(part, 'ind', from_ind(shift)))  3.85 us
    ppermute x3, starting transfers between devices, on_device(): lax.ppermute(block, ('dp', 'probe'), pairs)  3.55 us
    pallas_call x1, Pallas kernels, near_call(): pl.pallas_call(functools.partial(near_body, tile), out_shape=(pltpu.VMEM(...  3.55 us
    ppermute x1, starting transfers between devices, on_device(): stacks.append(lax.ppermute(stack, 'probe', from_group(shift)))  2.59 us
    pallas_call x1, Pallas kernels, far_call(): pl.pallas_call(functools.partial(far_body, tile_of(columns, 2048)), out_s...  2.48 us
    pallas_call x1, Pallas kernels, project_call(): pl.pallas_call(functools.partial(project_body, tile_of(columns, 2048)), o...  2.34 us
  transfers between devices with their start and end apart: 13, of which 6 were waited for; matrix products, arithmetic and copies ran while one was open for 0% of the time, Pallas kernels for 19%

profile of v4, /device:TPU:0, one launch (start us, length us, event | category | flops | bytes accessed | tf_op | source)
XLA Modules:
  0.0 37.0 jit_solution(2874540397821955048)
XLA Ops:
  0.0 0.5 %collective-permute-start.1 = (s32[8,16384]{1,0:T(8,128)}, s32[8,16384]{1,0:T(8,128)S(1)}, u32[]{:S(2)}, u32[]{:S(2)}) collective-permute-start(s32[8,16384]{1,0:T(8,128)} %signs_hbm.1), channel_id=1, source_target_pairs={{0,1},{1,0},{2,3},{3,2},{4,5},{5,4},{6,7},{7,6},{8,9},{9,8},{10,11... | collective-permute-start | bytes 1572872 | tf_op jit(solution)/shard_map/ppermute | solution.py:331
  0.5 0.0 collective-permute-start
  0.5 0.0 copy-start
  0.5 0.0 copy-start.1
  0.5 3.5 %kern_near.1 = (bf16[512,8192]{1,0:T(8,128)(2,1)S(1)}, bf16[16,8192]{1,0:T(8,128)(2,1)S(1)}, bf16[32,8192]{1,0:T(8,128)(2,1)S(1)}) custom-call(f32[1,16]{1,0:T(1,128)} %bitcast.7, bf16[16,512]{1,0:T(8,128)(2,1)} %refs_4_.1, bf16[16,16384]{1,0:T(8,128)(2,1)} %z_hbm.1, bf16[8,16384]{1,0:T(8,128)(2,1)} %solves_hbm.1, s32[8,16384]{1,0:T(8,128)} %signs_hbm.1), custom_call_target="tpu_custom_call" | custom-call | flops 1073741824 | bytes 8388608 | tf_op jit(solution)/shard_map/kern_near/pallas_call | solution.py:117
  4.1 0.0 collective-permute-done.solves_ref
  4.1 0.0 collective-permute-done.1.signs_ref
  4.1 0.1 stack.21.stack_ref.refs_0_
  4.2 2.3 %project.1 = (f32[16,512]{1,0:T(8,128)S(1)}, bf16[16,512]{1,0:T(8,128)(2,1)S(1)}) custom-call(bf16[512,8192]{1,0:T(8,128)(2,1)S(1)} %get-tuple-element.12.kern_ref.refs_6_, bf16[32,8192]{1,0:T(8,128)(2,1)S(1)} %stack.21.stack_ref.refs_0_), custom_call_target="tpu_custom_call" | custom-call | flops 268435456 | bytes 8388608 | tf_op jit(solution)/shard_map/project/pallas_call | solution.py:192
  6.5 0.5 %collective-permute-start.3 = (bf16[16,512]{1,0:T(8,128)(2,1)S(1)}, bf16[16,512]{1,0:T(8,128)(2,1)S(1)}, u32[]{:S(2)}, u32[]{:S(2)}) collective-permute-start(bf16[16,512]{1,0:T(8,128)(2,1)S(1)} %get-tuple-element.14), channel_id=1, source_target_pairs={{0,1},{1,0},{2,3},{3,2},{4,5},{5,4},{6,7},{7,6},{8,9},{9,8},{10,11... | collective-permute-start | bytes 49160 | tf_op jit(solution)/shard_map/ppermute | solution.py:331
  7.0 2.6 %collective-permute-start.2 = (bf16[32,8192]{1,0:T(8,128)(2,1)S(1)}, bf16[32,8192]{1,0:T(8,128)(2,1)S(1)}, u32[]{:S(2)}, u32[]{:S(2)}) collective-permute-start(bf16[32,8192]{1,0:T(8,128)(2,1)S(1)} %stack.21.stack_ref.refs_0_), channel_id=1, source_target_pairs={{2,0},{3,1},{0,2},{1,3},{6,4},{7,5},{4,6},{5,7},{10,8},{11,9},{8,1... | collective-permute-start | bytes 1572872 | tf_op jit(solution)/shard_map/ppermute | solution.py:353
  9.6 0.0 collective-permute-done.3
  9.6 3.7 %collective-permute-start.6 = (bf16[16,512]{1,0:T(8,128)(2,1)S(1)}, bf16[16,512]{1,0:T(8,128)(2,1)S(1)}, u32[]{:S(2)}, u32[]{:S(2)}) collective-permute-start(bf16[16,512]{1,0:T(8,128)(2,1)S(1)} %add_convert_fusion.1), channel_id=1, source_target_pairs={{12,0},{8,4},{4,8},{0,12},{13,1},{9,5},{5,9},{1,13},{14,2},{10,6},... | collective-permute-start | bytes 49160 | tf_op jit(solution)/shard_map/ppermute | solution.py:361
  13.3 0.0 collective-permute-start.5
  13.3 0.8 %collective-permute-start.4 = (bf16[16,512]{1,0:T(8,128)(2,1)S(1)}, bf16[16,512]{1,0:T(8,128)(2,1)S(1)}, u32[]{:S(2)}, u32[]{:S(2)}) collective-permute-start(bf16[16,512]{1,0:T(8,128)(2,1)S(1)} %add_convert_fusion.1), channel_id=1, source_target_pairs={{4,0},{0,4},{12,8},{8,12},{5,1},{1,5},{13,9},{9,13},{6,2},{2,6},{1... | collective-permute-start | bytes 49160 | tf_op jit(solution)/shard_map/ppermute | solution.py:361
  14.1 1.1 %collective-permute-done.6 = bf16[16,512]{1,0:T(8,128)(2,1)S(1)} collective-permute-done((bf16[16,512]{1,0:T(8,128)(2,1)S(1)}, bf16[16,512]{1,0:T(8,128)(2,1)S(1)}, u32[]{:S(2)}, u32[]{:S(2)}) %collective-permute-start.6) | collective-permute-done | bytes 16416 | tf_op jit(solution)/shard_map/ppermute | solution.py:361
  15.2 2.7 %collective-permute-done.5 = bf16[16,512]{1,0:T(8,128)(2,1)S(1)} collective-permute-done((bf16[16,512]{1,0:T(8,128)(2,1)S(1)}, bf16[16,512]{1,0:T(8,128)(2,1)S(1)}, u32[]{:S(2)}, u32[]{:S(2)}) %collective-permute-start.5) | collective-permute-done | bytes 16416 | tf_op jit(solution)/shard_map/ppermute | solution.py:361
  17.9 0.0 collective-permute-done.4
  17.9 2.0 %collective-permute-start.9 = (bf16[16,512]{1,0:T(8,128)(2,1)S(1)}, bf16[16,512]{1,0:T(8,128)(2,1)S(1)}, u32[]{:S(2)}, u32[]{:S(2)}) collective-permute-start(bf16[16,512]{1,0:T(8,128)(2,1)S(1)} %add_convert_fusion), channel_id=1, source_target_pairs={{18,0},{19,1},{16,2},{17,3},{2,16},{3,17},{0,18},{1,19},{22,4},{23... | collective-permute-start | bytes 49160 | tf_op jit(solution)/shard_map/ppermute | solution.py:371
  20.0 0.5 %collective-permute-start.8 = (bf16[16,512]{1,0:T(8,128)(2,1)S(1)}, bf16[16,512]{1,0:T(8,128)(2,1)S(1)}, u32[]{:S(2)}, u32[]{:S(2)}) collective-permute-start(bf16[16,512]{1,0:T(8,128)(2,1)S(1)} %add_convert_fusion), channel_id=1, source_target_pairs={{16,0},{17,1},{18,2},{19,3},{0,16},{1,17},{2,18},{3,19},{20,4},{21... | collective-permute-start | bytes 49160 | tf_op jit(solution)/shard_map/ppermute | solution.py:371
  20.5 1.0 %collective-permute-start.7 = (bf16[16,512]{1,0:T(8,128)(2,1)S(1)}, bf16[16,512]{1,0:T(8,128)(2,1)S(1)}, u32[]{:S(2)}, u32[]{:S(2)}) collective-permute-start(bf16[16,512]{1,0:T(8,128)(2,1)S(1)} %add_convert_fusion), channel_id=1, source_target_pairs={{2,0},{3,1},{0,2},{1,3},{18,16},{19,17},{16,18},{17,19},{6,4},{7,5... | collective-permute-start | bytes 49160 | tf_op jit(solution)/shard_map/ppermute | solution.py:371
  21.5 0.0 copy-done
  21.5 1.5 %collective-permute-start.11 = (bf16[16,512]{1,0:T(8,128)(2,1)S(1)}, bf16[16,512]{1,0:T(8,128)(2,1)S(1)}, u32[]{:S(2)}, u32[]{:S(2)}) collective-permute-start(bf16[16,512]{1,0:T(8,128)(2,1)S(1)} %copy-done), channel_id=1, source_target_pairs={{0,16},{16,0},{1,17},{17,1},{2,18},{18,2},{3,19},{19,3},{4,20},{20... | collective-permute-start | bytes 49160 | tf_op jit(solution)/shard_map/ppermute | solution.py:347
  23.6 0.0 collective-permute-done.9
  23.7 0.1 collective-permute-done.8
  23.7 0.5 %collective-permute-done.7 = bf16[16,512]{1,0:T(8,128)(2,1)S(1)} collective-permute-done((bf16[16,512]{1,0:T(8,128)(2,1)S(1)}, bf16[16,512]{1,0:T(8,128)(2,1)S(1)}, u32[]{:S(2)}, u32[]{:S(2)}) %collective-permute-start.7) | collective-permute-done | bytes 16416 | tf_op jit(solution)/shard_map/ppermute | solution.py:371
  24.3 0.1 collective-permute-start.10
  24.3 0.9 %collective-permute-done.11.x_ref.refs_5_ = bf16[16,512]{1,0:T(8,128)(2,1)S(1)} collective-permute-done((bf16[16,512]{1,0:T(8,128)(2,1)S(1)}, bf16[16,512]{1,0:T(8,128)(2,1)S(1)}, u32[]{:S(2)}, u32[]{:S(2)}) %collective-permute-start.11) | collective-permute-done | bytes 16416 | tf_op jit(solution)/shard_map/ppermute | solution.py:347
  25.2 0.0 copy-done.1
  25.2 2.5 %kern_far.1.refs_7_ = bf16[512,8192]{1,0:T(8,128)(2,1)S(1)} custom-call(f32[1,16]{1,0:T(1,128)S(1)} %bitcast.8, bf16[16,512]{1,0:T(8,128)(2,1)S(1)} %collective-permute-done.11.x_ref.refs_5_, bf16[16,8192]{1,0:T(8,128)(2,1)S(1)} %get-tuple-element.10.z_ref), custom_call_target="tpu_custom_call" | custom-call | flops 1073741824 | bytes 8388608 | tf_op jit(solution)/shard_map/kern_far/pallas_call | solution.py:141
  27.7 0.0 collective-permute-done.10.refs_3_
  27.7 0.0 collective-permute-done.2.refs_1_
  27.8 6.9 %gradient.1.grad_ref = bf16[16,8192]{1,0:T(8,128)(2,1)S(1)} custom-call(f32[1,1]{1,0:T(1,128)} %bitcast.6.noise_ref, f32[1,16]{1,0:T(1,128)S(1)} %bitcast.9, bf16[16,8192]{1,0:T(8,128)(2,1)S(1)} %get-tuple-element.10.z_ref, bf16[32,8192]{1,0:T(8,128)(2,1)S(1)} %stack.21.stack_ref.refs_0_, bf16[32,8192]{1,0:T(8,128)(2,1)S(1)} %collective-permute-done.2.refs_1_, ...), custom_call_target="tpu_custom_call" | custom-call | flops 2147483648 | bytes 16777216 | tf_op jit(solution)/shard_map/gradient/pallas_call | solution.py:276
  34.6 0.1 collective-permute-start.12
  34.7 0.8 %write_own.1.refs_0_ = f32[16,16384]{1,0:T(8,128)} custom-call(bf16[16,8192]{1,0:T(8,128)(2,1)S(1)} %gradient.1.grad_ref), custom_call_target="tpu_custom_call" | custom-call | flops 131072 | bytes 786432 | tf_op jit(solution)/shard_map/write_own/pallas_call | solution.py:310
  35.5 0.7 %collective-permute-done.12.grad_ref = bf16[16,8192]{1,0:T(8,128)(2,1)S(1)} collective-permute-done((bf16[16,8192]{1,0:T(8,128)(2,1)S(1)}, bf16[16,8192]{1,0:T(8,128)(2,1)S(1)}, u32[]{:S(2)}, u32[]{:S(2)}) %collective-permute-start.12) | collective-permute-done | bytes 262176 | tf_op jit(solution)/shard_map/ppermute | solution.py:331
  36.2 0.8 %write_other.1 = f32[16,16384]{1,0:T(8,128)} custom-call(bf16[16,8192]{1,0:T(8,128)(2,1)S(1)} %collective-permute-done.12.grad_ref, f32[16,16384]{1,0:T(8,128)} %write_own.1.refs_0_), custom_call_target="tpu_custom_call", output_to_operand_aliasing={{}: (1, {})} | custom-call | flops 131072 | bytes 786432 | tf_op jit(solution)/shard_map/write_other/pallas_call | solution.py:310
  (3 shorter events, 0.0 us)
Async XLA Ops:
  0.0 4.1 %collective-permute-start.1 = (s32[8,16384]{1,0:T(8,128)}, s32[8,16384]{1,0:T(8,128)S(1)}, u32[]{:S(2)}, u32[]{:S(2)}) collective-permute-start(s32[8,16384]{1,0:T(8,128)} %signs_hbm.1), channel_id=1, source_target_pairs={{0,1},{1,0},{2,3},{3,2},{4,5},{5,4},{6,7},{7,6},{8,9},{9,8},{10,11... | collective-permute-start | bytes 1572872 | tf_op jit(solution)/shard_map/ppermute | solution.py:331
  0.5 3.6 %collective-permute-start = (bf16[8,16384]{1,0:T(8,128)(2,1)}, bf16[8,16384]{1,0:T(8,128)(2,1)S(1)}, u32[]{:S(2)}, u32[]{:S(2)}) collective-permute-start(bf16[8,16384]{1,0:T(8,128)(2,1)} %solves_hbm.1), channel_id=1, source_target_pairs={{0,1},{1,0},{2,3},{3,2},{4,5},{5,4},{6,7},{7,6},{8,9},{9,8},{10,11... | collective-permute-start | bytes 786440 | tf_op jit(solution)/shard_map/ppermute | solution.py:331
  0.5 21.0 %copy-start = (bf16[16,512]{1,0:T(8,128)(2,1)S(1)}, bf16[16,512]{1,0:T(8,128)(2,1)}, u32[]{:S(2)}) copy-start(bf16[16,512]{1,0:T(8,128)(2,1)} %refs_4_.1) | copy-start | bytes 49156
  0.5 24.7 %copy-start.1 = (f32[16]{0:T(128)S(1)}, f32[16]{0:T(128)}, u32[]{:S(2)}) copy-start(f32[16]{0:T(128)} %param.8) | copy-start | bytes 196
  6.5 3.1 %collective-permute-start.3 = (bf16[16,512]{1,0:T(8,128)(2,1)S(1)}, bf16[16,512]{1,0:T(8,128)(2,1)S(1)}, u32[]{:S(2)}, u32[]{:S(2)}) collective-permute-start(bf16[16,512]{1,0:T(8,128)(2,1)S(1)} %get-tuple-element.14), channel_id=1, source_target_pairs={{0,1},{1,0},{2,3},{3,2},{4,5},{5,4},{6,7},{7,6},{8,9},{9,8},{10,11... | collective-permute-start | bytes 49160 | tf_op jit(solution)/shard_map/ppermute | solution.py:331
  7.0 20.7 %collective-permute-start.2 = (bf16[32,8192]{1,0:T(8,128)(2,1)S(1)}, bf16[32,8192]{1,0:T(8,128)(2,1)S(1)}, u32[]{:S(2)}, u32[]{:S(2)}) collective-permute-start(bf16[32,8192]{1,0:T(8,128)(2,1)S(1)} %stack.21.stack_ref.refs_0_), channel_id=1, source_target_pairs={{2,0},{3,1},{0,2},{1,3},{6,4},{7,5},{4,6},{5,7},{10,8},{11,9},{8,1... | collective-permute-start | bytes 1572872 | tf_op jit(solution)/shard_map/ppermute | solution.py:353
  9.6 5.6 %collective-permute-start.6 = (bf16[16,512]{1,0:T(8,128)(2,1)S(1)}, bf16[16,512]{1,0:T(8,128)(2,1)S(1)}, u32[]{:S(2)}, u32[]{:S(2)}) collective-permute-start(bf16[16,512]{1,0:T(8,128)(2,1)S(1)} %add_convert_fusion.1), channel_id=1, source_target_pairs={{12,0},{8,4},{4,8},{0,12},{13,1},{9,5},{5,9},{1,13},{14,2},{10,6},... | collective-permute-start | bytes 49160 | tf_op jit(solution)/shard_map/ppermute | solution.py:361
  13.3 4.6 %collective-permute-start.5 = (bf16[16,512]{1,0:T(8,128)(2,1)S(1)}, bf16[16,512]{1,0:T(8,128)(2,1)S(1)}, u32[]{:S(2)}, u32[]{:S(2)}) collective-permute-start(bf16[16,512]{1,0:T(8,128)(2,1)S(1)} %add_convert_fusion.1), channel_id=1, source_target_pairs={{8,0},{12,4},{0,8},{4,12},{9,1},{13,5},{1,9},{5,13},{10,2},{14,6},... | collective-permute-start | bytes 49160 | tf_op jit(solution)/shard_map/ppermute | solution.py:361
  13.3 4.6 %collective-permute-start.4 = (bf16[16,512]{1,0:T(8,128)(2,1)S(1)}, bf16[16,512]{1,0:T(8,128)(2,1)S(1)}, u32[]{:S(2)}, u32[]{:S(2)}) collective-permute-start(bf16[16,512]{1,0:T(8,128)(2,1)S(1)} %add_convert_fusion.1), channel_id=1, source_target_pairs={{4,0},{0,4},{12,8},{8,12},{5,1},{1,5},{13,9},{9,13},{6,2},{2,6},{1... | collective-permute-start | bytes 49160 | tf_op jit(solution)/shard_map/ppermute | solution.py:361
  17.9 5.7 %collective-permute-start.9 = (bf16[16,512]{1,0:T(8,128)(2,1)S(1)}, bf16[16,512]{1,0:T(8,128)(2,1)S(1)}, u32[]{:S(2)}, u32[]{:S(2)}) collective-permute-start(bf16[16,512]{1,0:T(8,128)(2,1)S(1)} %add_convert_fusion), channel_id=1, source_target_pairs={{18,0},{19,1},{16,2},{17,3},{2,16},{3,17},{0,18},{1,19},{22,4},{23... | collective-permute-start | bytes 49160 | tf_op jit(solution)/shard_map/ppermute | solution.py:371
  20.0 3.7 %collective-permute-start.8 = (bf16[16,512]{1,0:T(8,128)(2,1)S(1)}, bf16[16,512]{1,0:T(8,128)(2,1)S(1)}, u32[]{:S(2)}, u32[]{:S(2)}) collective-permute-start(bf16[16,512]{1,0:T(8,128)(2,1)S(1)} %add_convert_fusion), channel_id=1, source_target_pairs={{16,0},{17,1},{18,2},{19,3},{0,16},{1,17},{2,18},{3,19},{20,4},{21... | collective-permute-start | bytes 49160 | tf_op jit(solution)/shard_map/ppermute | solution.py:371
  20.5 3.7 %collective-permute-start.7 = (bf16[16,512]{1,0:T(8,128)(2,1)S(1)}, bf16[16,512]{1,0:T(8,128)(2,1)S(1)}, u32[]{:S(2)}, u32[]{:S(2)}) collective-permute-start(bf16[16,512]{1,0:T(8,128)(2,1)S(1)} %add_convert_fusion), channel_id=1, source_target_pairs={{2,0},{3,1},{0,2},{1,3},{18,16},{19,17},{16,18},{17,19},{6,4},{7,5... | collective-permute-start | bytes 49160 | tf_op jit(solution)/shard_map/ppermute | solution.py:371
  21.5 3.7 %collective-permute-start.11 = (bf16[16,512]{1,0:T(8,128)(2,1)S(1)}, bf16[16,512]{1,0:T(8,128)(2,1)S(1)}, u32[]{:S(2)}, u32[]{:S(2)}) collective-permute-start(bf16[16,512]{1,0:T(8,128)(2,1)S(1)} %copy-done), channel_id=1, source_target_pairs={{0,16},{16,0},{1,17},{17,1},{2,18},{18,2},{3,19},{19,3},{4,20},{20... | collective-permute-start | bytes 49160 | tf_op jit(solution)/shard_map/ppermute | solution.py:347
  24.3 3.5 %collective-permute-start.10 = (bf16[4,16,512]{2,1,0:T(8,128)(2,1)S(1)}, bf16[4,16,512]{2,1,0:T(8,128)(2,1)S(1)}, u32[]{:S(2)}, u32[]{:S(2)}) collective-permute-start(bf16[4,16,512]{2,1,0:T(8,128)(2,1)S(1)} %pad_maximum_fusion.refs_2_), channel_id=1, source_target_pairs={{0,1},{1,0},{2,3},{3,2},{4,5},{5,4},{6,7},{7,6},{8,9},{9,8},{10,11... | collective-permute-start | bytes 196616 | tf_op jit(solution)/shard_map/ppermute | solution.py:331
  34.6 1.6 %collective-permute-start.12 = (bf16[16,8192]{1,0:T(8,128)(2,1)S(1)}, bf16[16,8192]{1,0:T(8,128)(2,1)S(1)}, u32[]{:S(2)}, u32[]{:S(2)}) collective-permute-start(bf16[16,8192]{1,0:T(8,128)(2,1)S(1)} %gradient.1.grad_ref), channel_id=1, source_target_pairs={{0,1},{1,0},{2,3},{3,2},{4,5},{5,4},{6,7},{7,6},{8,9},{9,8},{10,11... | collective-permute-start | bytes 786440 | tf_op jit(solution)/shard_map/ppermute | solution.py:331

commit v5 on v4

--- a/solution.py
+++ b/solution.py
@@ -209,6 +209,7 @@
     groups, halves = len(stacks), len(kerns)
     columns = grad_ref.shape[1]
     count = kerns[0].shape[0]
+    piece = tile_of(count, 256)
     dims = data[0].shape[0]
     inverse = column(1.0 / length_ref[...])
     factor = inverse * inverse / (noise_ref[...] * p_size)
@@ -237,9 +238,11 @@
         target = slice(index * tile, (index + 1) * tile)
         stack = jnp.concatenate(in_order([ref[:, target].astype(F32) for ref in stacks]), axis=0).astype(BF16)
         for half in range(halves):
-            coef = jnp.dot(lefts[half], stack, preferred_element_type=F32)
-            weighted = (kerns[half][:, target].astype(F32) * coef).astype(BF16)
-            weighted_ref[index % 2, half * count : (half + 1) * count, :] = weighted
+            for start in range(0, count, piece):
+                part = slice(start, start + piece)
+                coef = jnp.dot(lefts[half][part], stack, preferred_element_type=F32)
+                weighted = (kerns[half][part, target].astype(F32) * coef).astype(BF16)
+                weighted_ref[index % 2, half * count + start : half * count + start + piece, :] = weighted
 
     def reduce(index):
         target = slice(index * tile, (index + 1) * tile)

time: 37.2 us -> 37.3 us (level)
  transfers between devices with their start and end apart: 13 -> 13, of which waited for: 6 -> 6; matrix products, arithmetic and copies ran while one was open for 0% -> 0% of each run, Pallas kernels for 19% -> 18%
where the time goes in v5:
time: 37.3 us; the launch traced here: 37.2 us
  Pallas kernels  17.1 us (46%)
  starting transfers between devices  13.2 us (35%)
  waiting for transfers between devices  6.04 us (16%)
  between operations  0.76 us (2%)
    pallas_call x1, Pallas kernels, gradient_call(): pl.pallas_call(body, out_shape=jax.ShapeDtypeStruct(z.shape, dtype), in_s...  7.04 us
    ppermute x3, starting transfers between devices, on_device(): peers.append(lax.ppermute(part, 'ind', from_ind(shift)))  4.45 us
    ppermute x3, waiting for transfers between devices, on_device(): peers.append(lax.ppermute(part, 'ind', from_ind(shift)))  3.85 us
    ppermute x3, starting transfers between devices, on_device(): lax.ppermute(block, ('dp', 'probe'), pairs)  3.55 us
    pallas_call x1, Pallas kernels, near_call(): pl.pallas_call(functools.partial(near_body, tile), out_shape=(pltpu.VMEM(...  3.55 us
    ppermute x1, starting transfers between devices, on_device(): stacks.append(lax.ppermute(stack, 'probe', from_group(shift)))  2.59 us
    pallas_call x1, Pallas kernels, far_call(): pl.pallas_call(functools.partial(far_body, tile_of(columns, 2048)), out_s...  2.48 us
    pallas_call x1, Pallas kernels, project_call(): pl.pallas_call(functools.partial(project_body, tile_of(columns, 2048)), o...  2.34 us
  transfers between devices with their start and end apart: 13, of which 6 were waited for; matrix products, arithmetic and copies ran while one was open for 0% of the time, Pallas kernels for 18%

profile of v5, /device:TPU:0, one launch (start us, length us, event | category | flops | bytes accessed | tf_op | source)
XLA Modules:
  0.0 37.2 jit_solution(2005501592451956389)
XLA Ops:
  0.0 0.5 %collective-permute-start.1 = (s32[8,16384]{1,0:T(8,128)}, s32[8,16384]{1,0:T(8,128)S(1)}, u32[]{:S(2)}, u32[]{:S(2)}) collective-permute-start(s32[8,16384]{1,0:T(8,128)} %signs_hbm.1), channel_id=1, source_target_pairs={{0,1},{1,0},{2,3},{3,2},{4,5},{5,4},{6,7},{7,6},{8,9},{9,8},{10,11... | collective-permute-start | bytes 1572872 | tf_op jit(solution)/shard_map/ppermute | solution.py:334
  0.5 0.0 collective-permute-start
  0.5 0.0 copy-start
  0.5 0.0 copy-start.1
  0.5 3.5 %kern_near.1 = (bf16[512,8192]{1,0:T(8,128)(2,1)S(1)}, bf16[16,8192]{1,0:T(8,128)(2,1)S(1)}, bf16[32,8192]{1,0:T(8,128)(2,1)S(1)}) custom-call(f32[1,16]{1,0:T(1,128)} %bitcast.7, bf16[16,512]{1,0:T(8,128)(2,1)} %refs_4_.1, bf16[16,16384]{1,0:T(8,128)(2,1)} %z_hbm.1, bf16[8,16384]{1,0:T(8,128)(2,1)} %solves_hbm.1, s32[8,16384]{1,0:T(8,128)} %signs_hbm.1), custom_call_target="tpu_custom_call" | custom-call | flops 1073741824 | bytes 8388608 | tf_op jit(solution)/shard_map/kern_near/pallas_call | solution.py:117
  4.1 0.0 collective-permute-done.solves_ref
  4.1 0.0 collective-permute-done.1.signs_ref
  4.1 0.1 stack.21.stack_ref.refs_0_
  4.2 2.3 %project.1 = (f32[16,512]{1,0:T(8,128)S(1)}, bf16[16,512]{1,0:T(8,128)(2,1)S(1)}) custom-call(bf16[512,8192]{1,0:T(8,128)(2,1)S(1)} %get-tuple-element.12.kern_ref.refs_6_, bf16[32,8192]{1,0:T(8,128)(2,1)S(1)} %stack.21.stack_ref.refs_0_), custom_call_target="tpu_custom_call" | custom-call | flops 268435456 | bytes 8388608 | tf_op jit(solution)/shard_map/project/pallas_call | solution.py:192
  6.5 0.5 %collective-permute-start.3 = (bf16[16,512]{1,0:T(8,128)(2,1)S(1)}, bf16[16,512]{1,0:T(8,128)(2,1)S(1)}, u32[]{:S(2)}, u32[]{:S(2)}) collective-permute-start(bf16[16,512]{1,0:T(8,128)(2,1)S(1)} %get-tuple-element.14), channel_id=1, source_target_pairs={{0,1},{1,0},{2,3},{3,2},{4,5},{5,4},{6,7},{7,6},{8,9},{9,8},{10,11... | collective-permute-start | bytes 49160 | tf_op jit(solution)/shard_map/ppermute | solution.py:334
  7.0 2.6 %collective-permute-start.2 = (bf16[32,8192]{1,0:T(8,128)(2,1)S(1)}, bf16[32,8192]{1,0:T(8,128)(2,1)S(1)}, u32[]{:S(2)}, u32[]{:S(2)}) collective-permute-start(bf16[32,8192]{1,0:T(8,128)(2,1)S(1)} %stack.21.stack_ref.refs_0_), channel_id=1, source_target_pairs={{2,0},{3,1},{0,2},{1,3},{6,4},{7,5},{4,6},{5,7},{10,8},{11,9},{8,1... | collective-permute-start | bytes 1572872 | tf_op jit(solution)/shard_map/ppermute | solution.py:356
  9.6 0.0 collective-permute-done.3
  9.6 3.7 %collective-permute-start.6 = (bf16[16,512]{1,0:T(8,128)(2,1)S(1)}, bf16[16,512]{1,0:T(8,128)(2,1)S(1)}, u32[]{:S(2)}, u32[]{:S(2)}) collective-permute-start(bf16[16,512]{1,0:T(8,128)(2,1)S(1)} %add_convert_fusion.1), channel_id=1, source_target_pairs={{12,0},{8,4},{4,8},{0,12},{13,1},{9,5},{5,9},{1,13},{14,2},{10,6},... | collective-permute-start | bytes 49160 | tf_op jit(solution)/shard_map/ppermute | solution.py:364
  13.3 0.0 collective-permute-start.5
  13.3 0.8 %collective-permute-start.4 = (bf16[16,512]{1,0:T(8,128)(2,1)S(1)}, bf16[16,512]{1,0:T(8,128)(2,1)S(1)}, u32[]{:S(2)}, u32[]{:S(2)}) collective-permute-start(bf16[16,512]{1,0:T(8,128)(2,1)S(1)} %add_convert_fusion.1), channel_id=1, source_target_pairs={{4,0},{0,4},{12,8},{8,12},{5,1},{1,5},{13,9},{9,13},{6,2},{2,6},{1... | collective-permute-start | bytes 49160 | tf_op jit(solution)/shard_map/ppermute | solution.py:364
  14.1 1.1 %collective-permute-done.6 = bf16[16,512]{1,0:T(8,128)(2,1)S(1)} collective-permute-done((bf16[16,512]{1,0:T(8,128)(2,1)S(1)}, bf16[16,512]{1,0:T(8,128)(2,1)S(1)}, u32[]{:S(2)}, u32[]{:S(2)}) %collective-permute-start.6) | collective-permute-done | bytes 16416 | tf_op jit(solution)/shard_map/ppermute | solution.py:364
  15.2 2.7 %collective-permute-done.5 = bf16[16,512]{1,0:T(8,128)(2,1)S(1)} collective-permute-done((bf16[16,512]{1,0:T(8,128)(2,1)S(1)}, bf16[16,512]{1,0:T(8,128)(2,1)S(1)}, u32[]{:S(2)}, u32[]{:S(2)}) %collective-permute-start.5) | collective-permute-done | bytes 16416 | tf_op jit(solution)/shard_map/ppermute | solution.py:364
  17.9 0.0 collective-permute-done.4
  17.9 2.0 %collective-permute-start.9 = (bf16[16,512]{1,0:T(8,128)(2,1)S(1)}, bf16[16,512]{1,0:T(8,128)(2,1)S(1)}, u32[]{:S(2)}, u32[]{:S(2)}) collective-permute-start(bf16[16,512]{1,0:T(8,128)(2,1)S(1)} %add_convert_fusion), channel_id=1, source_target_pairs={{18,0},{19,1},{16,2},{17,3},{2,16},{3,17},{0,18},{1,19},{22,4},{23... | collective-permute-start | bytes 49160 | tf_op jit(solution)/shard_map/ppermute | solution.py:374
  20.0 0.5 %collective-permute-start.8 = (bf16[16,512]{1,0:T(8,128)(2,1)S(1)}, bf16[16,512]{1,0:T(8,128)(2,1)S(1)}, u32[]{:S(2)}, u32[]{:S(2)}) collective-permute-start(bf16[16,512]{1,0:T(8,128)(2,1)S(1)} %add_convert_fusion), channel_id=1, source_target_pairs={{16,0},{17,1},{18,2},{19,3},{0,16},{1,17},{2,18},{3,19},{20,4},{21... | collective-permute-start | bytes 49160 | tf_op jit(solution)/shard_map/ppermute | solution.py:374
  20.5 1.0 %collective-permute-start.7 = (bf16[16,512]{1,0:T(8,128)(2,1)S(1)}, bf16[16,512]{1,0:T(8,128)(2,1)S(1)}, u32[]{:S(2)}, u32[]{:S(2)}) collective-permute-start(bf16[16,512]{1,0:T(8,128)(2,1)S(1)} %add_convert_fusion), channel_id=1, source_target_pairs={{2,0},{3,1},{0,2},{1,3},{18,16},{19,17},{16,18},{17,19},{6,4},{7,5... | collective-permute-start | bytes 49160 | tf_op jit(solution)/shard_map/ppermute | solution.py:374
  21.5 0.0 copy-done
  21.5 1.5 %collective-permute-start.11 = (bf16[16,512]{1,0:T(8,128)(2,1)S(1)}, bf16[16,512]{1,0:T(8,128)(2,1)S(1)}, u32[]{:S(2)}, u32[]{:S(2)}) collective-permute-start(bf16[16,512]{1,0:T(8,128)(2,1)S(1)} %copy-done), channel_id=1, source_target_pairs={{0,16},{16,0},{1,17},{17,1},{2,18},{18,2},{3,19},{19,3},{4,20},{20... | collective-permute-start | bytes 49160 | tf_op jit(solution)/shard_map/ppermute | solution.py:350
  23.6 0.0 collective-permute-done.9
  23.7 0.1 collective-permute-done.8
  23.7 0.5 %collective-permute-done.7 = bf16[16,512]{1,0:T(8,128)(2,1)S(1)} collective-permute-done((bf16[16,512]{1,0:T(8,128)(2,1)S(1)}, bf16[16,512]{1,0:T(8,128)(2,1)S(1)}, u32[]{:S(2)}, u32[]{:S(2)}) %collective-permute-start.7) | collective-permute-done | bytes 16416 | tf_op jit(solution)/shard_map/ppermute | solution.py:374
  24.3 0.1 collective-permute-start.10
  24.3 0.9 %collective-permute-done.11.x_ref.refs_5_ = bf16[16,512]{1,0:T(8,128)(2,1)S(1)} collective-permute-done((bf16[16,512]{1,0:T(8,128)(2,1)S(1)}, bf16[16,512]{1,0:T(8,128)(2,1)S(1)}, u32[]{:S(2)}, u32[]{:S(2)}) %collective-permute-start.11) | collective-permute-done | bytes 16416 | tf_op jit(solution)/shard_map/ppermute | solution.py:350
  25.2 0.0 copy-done.1
  25.2 2.5 %kern_far.1.refs_7_ = bf16[512,8192]{1,0:T(8,128)(2,1)S(1)} custom-call(f32[1,16]{1,0:T(1,128)S(1)} %bitcast.8, bf16[16,512]{1,0:T(8,128)(2,1)S(1)} %collective-permute-done.11.x_ref.refs_5_, bf16[16,8192]{1,0:T(8,128)(2,1)S(1)} %get-tuple-element.10.z_ref), custom_call_target="tpu_custom_call" | custom-call | flops 1073741824 | bytes 8388608 | tf_op jit(solution)/shard_map/kern_far/pallas_call | solution.py:141
  27.7 0.0 collective-permute-done.10.refs_3_
  27.7 0.0 collective-permute-done.2.refs_1_
  27.8 7.0 %gradient.1.grad_ref = bf16[16,8192]{1,0:T(8,128)(2,1)S(1)} custom-call(f32[1,1]{1,0:T(1,128)} %bitcast.6.noise_ref, f32[1,16]{1,0:T(1,128)S(1)} %bitcast.9, bf16[16,8192]{1,0:T(8,128)(2,1)S(1)} %get-tuple-element.10.z_ref, bf16[32,8192]{1,0:T(8,128)(2,1)S(1)} %stack.21.stack_ref.refs_0_, bf16[32,8192]{1,0:T(8,128)(2,1)S(1)} %collective-permute-done.2.refs_1_, ...), custom_call_target="tpu_custom_call" | custom-call | flops 2147483648 | bytes 16777216 | tf_op jit(solution)/shard_map/gradient/pallas_call | solution.py:279
  34.8 0.0 collective-permute-start.12
  34.8 0.8 %write_own.1.refs_0_ = f32[16,16384]{1,0:T(8,128)} custom-call(bf16[16,8192]{1,0:T(8,128)(2,1)S(1)} %gradient.1.grad_ref), custom_call_target="tpu_custom_call" | custom-call | flops 131072 | bytes 786432 | tf_op jit(solution)/shard_map/write_own/pallas_call | solution.py:313
  35.7 0.7 %collective-permute-done.12.grad_ref = bf16[16,8192]{1,0:T(8,128)(2,1)S(1)} collective-permute-done((bf16[16,8192]{1,0:T(8,128)(2,1)S(1)}, bf16[16,8192]{1,0:T(8,128)(2,1)S(1)}, u32[]{:S(2)}, u32[]{:S(2)}) %collective-permute-start.12) | collective-permute-done | bytes 262176 | tf_op jit(solution)/shard_map/ppermute | solution.py:334
  36.3 0.8 %write_other.1 = f32[16,16384]{1,0:T(8,128)} custom-call(bf16[16,8192]{1,0:T(8,128)(2,1)S(1)} %collective-permute-done.12.grad_ref, f32[16,16384]{1,0:T(8,128)} %write_own.1.refs_0_), custom_call_target="tpu_custom_call", output_to_operand_aliasing={{}: (1, {})} | custom-call | flops 131072 | bytes 786432 | tf_op jit(solution)/shard_map/write_other/pallas_call | solution.py:313
  (3 shorter events, 0.0 us)
Async XLA Ops:
  0.0 4.1 %collective-permute-start.1 = (s32[8,16384]{1,0:T(8,128)}, s32[8,16384]{1,0:T(8,128)S(1)}, u32[]{:S(2)}, u32[]{:S(2)}) collective-permute-start(s32[8,16384]{1,0:T(8,128)} %signs_hbm.1), channel_id=1, source_target_pairs={{0,1},{1,0},{2,3},{3,2},{4,5},{5,4},{6,7},{7,6},{8,9},{9,8},{10,11... | collective-permute-start | bytes 1572872 | tf_op jit(solution)/shard_map/ppermute | solution.py:334
  0.5 3.6 %collective-permute-start = (bf16[8,16384]{1,0:T(8,128)(2,1)}, bf16[8,16384]{1,0:T(8,128)(2,1)S(1)}, u32[]{:S(2)}, u32[]{:S(2)}) collective-permute-start(bf16[8,16384]{1,0:T(8,128)(2,1)} %solves_hbm.1), channel_id=1, source_target_pairs={{0,1},{1,0},{2,3},{3,2},{4,5},{5,4},{6,7},{7,6},{8,9},{9,8},{10,11... | collective-permute-start | bytes 786440 | tf_op jit(solution)/shard_map/ppermute | solution.py:334
  0.5 21.0 %copy-start = (bf16[16,512]{1,0:T(8,128)(2,1)S(1)}, bf16[16,512]{1,0:T(8,128)(2,1)}, u32[]{:S(2)}) copy-start(bf16[16,512]{1,0:T(8,128)(2,1)} %refs_4_.1) | copy-start | bytes 49156
  0.5 24.7 %copy-start.1 = (f32[16]{0:T(128)S(1)}, f32[16]{0:T(128)}, u32[]{:S(2)}) copy-start(f32[16]{0:T(128)} %param.8) | copy-start | bytes 196
  6.5 3.1 %collective-permute-start.3 = (bf16[16,512]{1,0:T(8,128)(2,1)S(1)}, bf16[16,512]{1,0:T(8,128)(2,1)S(1)}, u32[]{:S(2)}, u32[]{:S(2)}) collective-permute-start(bf16[16,512]{1,0:T(8,128)(2,1)S(1)} %get-tuple-element.14), channel_id=1, source_target_pairs={{0,1},{1,0},{2,3},{3,2},{4,5},{5,4},{6,7},{7,6},{8,9},{9,8},{10,11... | collective-permute-start | bytes 49160 | tf_op jit(solution)/shard_map/ppermute | solution.py:334
  7.0 20.7 %collective-permute-start.2 = (bf16[32,8192]{1,0:T(8,128)(2,1)S(1)}, bf16[32,8192]{1,0:T(8,128)(2,1)S(1)}, u32[]{:S(2)}, u32[]{:S(2)}) collective-permute-start(bf16[32,8192]{1,0:T(8,128)(2,1)S(1)} %stack.21.stack_ref.refs_0_), channel_id=1, source_target_pairs={{2,0},{3,1},{0,2},{1,3},{6,4},{7,5},{4,6},{5,7},{10,8},{11,9},{8,1... | collective-permute-start | bytes 1572872 | tf_op jit(solution)/shard_map/ppermute | solution.py:356
  9.6 5.6 %collective-permute-start.6 = (bf16[16,512]{1,0:T(8,128)(2,1)S(1)}, bf16[16,512]{1,0:T(8,128)(2,1)S(1)}, u32[]{:S(2)}, u32[]{:S(2)}) collective-permute-start(bf16[16,512]{1,0:T(8,128)(2,1)S(1)} %add_convert_fusion.1), channel_id=1, source_target_pairs={{12,0},{8,4},{4,8},{0,12},{13,1},{9,5},{5,9},{1,13},{14,2},{10,6},... | collective-permute-start | bytes 49160 | tf_op jit(solution)/shard_map/ppermute | solution.py:364
  13.3 4.6 %collective-permute-start.5 = (bf16[16,512]{1,0:T(8,128)(2,1)S(1)}, bf16[16,512]{1,0:T(8,128)(2,1)S(1)}, u32[]{:S(2)}, u32[]{:S(2)}) collective-permute-start(bf16[16,512]{1,0:T(8,128)(2,1)S(1)} %add_convert_fusion.1), channel_id=1, source_target_pairs={{8,0},{12,4},{0,8},{4,12},{9,1},{13,5},{1,9},{5,13},{10,2},{14,6},... | collective-permute-start | bytes 49160 | tf_op jit(solution)/shard_map/ppermute | solution.py:364
  13.3 4.6 %collective-permute-start.4 = (bf16[16,512]{1,0:T(8,128)(2,1)S(1)}, bf16[16,512]{1,0:T(8,128)(2,1)S(1)}, u32[]{:S(2)}, u32[]{:S(2)}) collective-permute-start(bf16[16,512]{1,0:T(8,128)(2,1)S(1)} %add_convert_fusion.1), channel_id=1, source_target_pairs={{4,0},{0,4},{12,8},{8,12},{5,1},{1,5},{13,9},{9,13},{6,2},{2,6},{1... | collective-permute-start | bytes 49160 | tf_op jit(solution)/shard_map/ppermute | solution.py:364
  17.9 5.7 %collective-permute-start.9 = (bf16[16,512]{1,0:T(8,128)(2,1)S(1)}, bf16[16,512]{1,0:T(8,128)(2,1)S(1)}, u32[]{:S(2)}, u32[]{:S(2)}) collective-permute-start(bf16[16,512]{1,0:T(8,128)(2,1)S(1)} %add_convert_fusion), channel_id=1, source_target_pairs={{18,0},{19,1},{16,2},{17,3},{2,16},{3,17},{0,18},{1,19},{22,4},{23... | collective-permute-start | bytes 49160 | tf_op jit(solution)/shard_map/ppermute | solution.py:374
  20.0 3.7 %collective-permute-start.8 = (bf16[16,512]{1,0:T(8,128)(2,1)S(1)}, bf16[16,512]{1,0:T(8,128)(2,1)S(1)}, u32[]{:S(2)}, u32[]{:S(2)}) collective-permute-start(bf16[16,512]{1,0:T(8,128)(2,1)S(1)} %add_convert_fusion), channel_id=1, source_target_pairs={{16,0},{17,1},{18,2},{19,3},{0,16},{1,17},{2,18},{3,19},{20,4},{21... | collective-permute-start | bytes 49160 | tf_op jit(solution)/shard_map/ppermute | solution.py:374
  20.5 3.7 %collective-permute-start.7 = (bf16[16,512]{1,0:T(8,128)(2,1)S(1)}, bf16[16,512]{1,0:T(8,128)(2,1)S(1)}, u32[]{:S(2)}, u32[]{:S(2)}) collective-permute-start(bf16[16,512]{1,0:T(8,128)(2,1)S(1)} %add_convert_fusion), channel_id=1, source_target_pairs={{2,0},{3,1},{0,2},{1,3},{18,16},{19,17},{16,18},{17,19},{6,4},{7,5... | collective-permute-start | bytes 49160 | tf_op jit(solution)/shard_map/ppermute | solution.py:374
  21.5 3.7 %collective-permute-start.11 = (bf16[16,512]{1,0:T(8,128)(2,1)S(1)}, bf16[16,512]{1,0:T(8,128)(2,1)S(1)}, u32[]{:S(2)}, u32[]{:S(2)}) collective-permute-start(bf16[16,512]{1,0:T(8,128)(2,1)S(1)} %copy-done), channel_id=1, source_target_pairs={{0,16},{16,0},{1,17},{17,1},{2,18},{18,2},{3,19},{19,3},{4,20},{20... | collective-permute-start | bytes 49160 | tf_op jit(solution)/shard_map/ppermute | solution.py:350
  24.3 3.5 %collective-permute-start.10 = (bf16[4,16,512]{2,1,0:T(8,128)(2,1)S(1)}, bf16[4,16,512]{2,1,0:T(8,128)(2,1)S(1)}, u32[]{:S(2)}, u32[]{:S(2)}) collective-permute-start(bf16[4,16,512]{2,1,0:T(8,128)(2,1)S(1)} %pad_maximum_fusion.refs_2_), channel_id=1, source_target_pairs={{0,1},{1,0},{2,3},{3,2},{4,5},{5,4},{6,7},{7,6},{8,9},{9,8},{10,11... | collective-permute-start | bytes 196616 | tf_op jit(solution)/shard_map/ppermute | solution.py:334
  34.8 1.6 %collective-permute-start.12 = (bf16[16,8192]{1,0:T(8,128)(2,1)S(1)}, bf16[16,8192]{1,0:T(8,128)(2,1)S(1)}, u32[]{:S(2)}, u32[]{:S(2)}) collective-permute-start(bf16[16,8192]{1,0:T(8,128)(2,1)S(1)} %gradient.1.grad_ref), channel_id=1, source_target_pairs={{0,1},{1,0},{2,3},{3,2},{4,5},{5,4},{6,7},{7,6},{8,9},{9,8},{10,11... | collective-permute-start | bytes 786440 | tf_op jit(solution)/shard_map/ppermute | solution.py:334
